TPU v7x, 256 devices: a whole 4x4x8 slice. The times are simulated.
256 devices in a mesh: row: 64 (over x, z, core), col: 4 (over y).
Axes of the slice: x: 4, y: 4, z: 8, core: 2. Of those that a mesh axis runs over, the one named last changes fastest.
Arguments:
- pivot_block: float32 [512, 512], P('row', 'col'), as said below
- pivot_tangent: float32 [512, 512], P('row', 'col'), as said below
- panel_block: float32 [65536, 512], P('row', 'col'), may hold values from -1.5 to 1.5
- panel_tangent: float32 [65536, 512], P('row', 'col'), may hold values from -1.5 to 1.5
- strip_block: float32 [65536, 2048], P('row', 'col'), may hold values from -6 to 6
- strip_tangent: float32 [65536, 2048], P('row', 'col'), may hold values from -6 to 6
Outputs:
- pivot_factor: float32 [512, 512], P('row', 'col')
- pivot_factor_tangent: float32 [512, 512], P('row', 'col')
- panel_factor: float32 [65536, 512], P('row', 'col')
- panel_factor_tangent: float32 [65536, 512], P('row', 'col')
- strip_updated: float32 [65536, 2048], P('row', 'col')
- strip_updated_tangent: float32 [65536, 2048], P('row', 'col')
Inputs may be any that keep to these rules, and one draw needn't show every extreme that they name: `pivot_block`: symmetric positive definite; its smallest eigenvalue is at least 0.05. `pivot_tangent`: symmetric.
All inputs are finite; a program needn't handle non-finite values.
Results may differ from a plain program's by a relative error of at most 0.0003.
Values sent between devices are 32-bit elements; how exact they have to be, the bound alone decides.
No kernel may reach another device: no remote copies, remote signals or barrier semaphores. Data moves between devices by JAX's collectives and lax.ppermute only.
A program may use at most 128 MiB of HBM per device.

v0:
```python
import jax
import jax.numpy as jnp
from jax import lax
from jax.experimental import pallas as pl
from jax.experimental.pallas import tpu as pltpu
from jax.sharding import PartitionSpec as P

PIVOT = 512
HALF = PIVOT // 2
BLOCK = 64
PANEL_TILE = 256
F32 = jnp.float32
BF16 = jnp.bfloat16
N_X, N_Z, N_CORE, N_Y = 4, 8, 2, 4


def exact_nt(a, b):
    return lax.dot_general(
        a, b, (((1,), (1,)), ((), ())), precision=lax.Precision.HIGHEST, preferred_element_type=F32
    )


def exact_nn(a, b):
    return lax.dot_general(
        a, b, (((1,), (0,)), ((), ())), precision=lax.Precision.HIGHEST, preferred_element_type=F32
    )


def halves(x):
    high = x.astype(BF16)
    return high, (x - high.astype(F32)).astype(BF16)


def nt(a, b):
    return lax.dot_general(a, b, (((1,), (1,)), ((), ())), preferred_element_type=F32)


def split_nt(a, b):
    return nt(a[0], b[0]) + (nt(a[0], b[1]) + nt(a[1], b[0]))


def lane(x, k):
    return jnp.broadcast_to(x[:, k : k + 1], (8, 128))


def sub(x, k):
    return jnp.broadcast_to(x[k : k + 1, :], (8, 128))


def factor_block(rows):
    rows = list(rows)
    sublane = lax.broadcasted_iota(jnp.int32, (8, 128), 0)
    done = []
    for s in range(8):
        cols = {b: [lane(rows[b], 8 * s + k) for k in range(8)] for b in range(s, 8)}
        corner = [[sub(cols[s][k], i) if i >= k else None for k in range(8)] for i in range(8)]
        scale = None
        for k in range(8):
            r = 1.0 / corner[k][k]
            m = [corner[i][k] * r if i > k else None for i in range(8)]
            for i in range(k + 1, 8):
                for j in range(k + 1, i + 1):
                    corner[i][j] = corner[i][j] - m[i] * corner[j][k]
            pivot_row = sub(rows[s], k)
            for b in range(s, 8):
                mul = cols[b][k] * r
                if b == s:
                    mul = jnp.where(sublane > k, mul, 0.0)
                for j in range(k + 1, 8):
                    cols[b][j] = cols[b][j] - mul * corner[j][k]
                rows[b] = rows[b] - mul * pivot_row
            y = lax.rsqrt(corner[k][k])
            y = y * (1.5 - 0.5 * corner[k][k] * y * y)
            scale = y if scale is None else jnp.where(sublane == k, y, scale)
        done.append(rows[s] * scale)
    return done


def merge(l_ref, x_ref, lo, h):
    a, b, c = lo, lo + h, lo + 2 * h
    t = exact_nn(l_ref[b:c, a:b], x_ref[a:b, a:b])
    x_ref[b:c, a:b] = -exact_nn(x_ref[b:c, b:c], t)


def forward(w_ref, l_ref, x_ref, lo, h):
    a, b, c = lo, lo + h, lo + 2 * h
    l21 = exact_nt(w_ref[b:c, a:b], x_ref[a:b, a:b])
    l_ref[b:c, a:b] = l21
    w_ref[b:c, b:c] = w_ref[b:c, b:c] - exact_nt(l21, l21)


def after_block(w_ref, l_ref, x_ref, j):
    h = BLOCK
    while h < HALF:
        if j % 2 == 1:
            merge(l_ref, x_ref, (j - 1) * h, h)
            j //= 2
            h *= 2
        else:
            forward(w_ref, l_ref, x_ref, j * h, h)
            return


def factor_blocks(w_ref, l_ref, x_ref, first, last):
    ri = lax.broadcasted_iota(jnp.int32, (BLOCK, BLOCK), 0)
    ci = lax.broadcasted_iota(jnp.int32, (BLOCK, BLOCK), 1)
    wide = lax.broadcasted_iota(jnp.int32, (BLOCK, 128), 1)
    eye = jnp.where(ri == ci, 1.0, 0.0).astype(F32)
    zero = jnp.zeros((BLOCK, BLOCK), F32)

    def step(j, carry):
        rows = pl.ds(pl.multiple_of(j * BLOCK, BLOCK), BLOCK)
        lanes = pl.ds(pl.multiple_of((j // 2) * 128, 128), 128)
        full = w_ref[rows, lanes]
        d = jnp.where(j % 2 == 0, full[:, :BLOCK], full[:, BLOCK:])
        both = jnp.concatenate([d, eye], axis=1)
        both = factor_block([both[8 * b : 8 * b + 8] for b in range(8)])
        both = jnp.concatenate(both, axis=0)
        low = jnp.where(ri >= ci, both[:, :BLOCK].T, 0.0)
        inverse = jnp.where(ri >= ci, both[:, BLOCK:], 0.0)
        for side in range(2):

            @pl.when(j % 2 == side)
            def _():
                put = lambda v: jnp.concatenate([v, zero] if side == 0 else [zero, v], 1)
                x_ref[rows, lanes] = put(inverse)
                l_ref[rows, lanes] = jnp.where(wide >= side * BLOCK, put(low), l_ref[rows, lanes])

        for jj in range(first, last):

            @pl.when(j == jj)
            def _():
                after_block(w_ref, l_ref, x_ref, jj)

        return carry

    lax.fori_loop(first, last, step, 0)


def col_lanes(at_ref):
    col = at_ref[1]
    return [pl.ds(pl.multiple_of(lax.rem(col + N_Y - s, N_Y) * 128, 128), 128) for s in range(N_Y)]


def spread(at_ref, pieces, at_tile, out_ref):
    x, core = at_ref[2], at_ref[3]
    lanes = col_lanes(at_ref)
    for s_core in range(N_CORE):
        for s_x in range(N_X):
            piece = pieces[s_core * N_X + s_x]
            first = lax.rem(x + N_X - s_x, N_X) * N_Z * N_CORE + lax.rem(core + s_core, N_CORE)
            for z in range(N_Z):
                rows = pl.ds(pl.multiple_of((first + z * N_CORE) * 8, 8), 8)
                for s_y in range(N_Y):
                    out_ref[rows, lanes[s_y]] = piece[(z, s_y) + at_tile]


def first_half(*refs):
    at_ref, pieces = refs[0], refs[1:9]
    w_out, l_ref, x_ref, w_ref = refs[9:]
    spread(at_ref, pieces, (), w_ref)
    l_ref[...] = jnp.zeros((PIVOT, HALF), F32)
    x_ref[...] = jnp.zeros((HALF, HALF), F32)
    factor_blocks(w_ref, l_ref, x_ref, 0, HALF // BLOCK)
    a = slice(0, HALF)
    b = slice(HALF, PIVOT)
    l21 = exact_nt(w_ref[b, a], x_ref[...])
    l_ref[b, :] = l21
    w_out[...] = w_ref[b, b] - exact_nt(l21, l21)


def second_half(w_in, l_in, x_in, l_ref, x_ref, w_ref, l22, x22):
    a = slice(0, HALF)
    b = slice(HALF, PIVOT)
    w_ref[...] = w_in[...]
    l22[...] = jnp.zeros((HALF, HALF), F32)
    x22[...] = jnp.zeros((HALF, HALF), F32)
    factor_blocks(w_ref, l22, x22, 0, HALF // BLOCK)
    l_ref[:, a] = l_in[...]
    l_ref[a, b] = jnp.zeros((HALF, HALF), F32)
    l_ref[b, b] = l22[...]
    x_ref[a, a] = x_in[...]
    x_ref[a, b] = jnp.zeros((HALF, HALF), F32)
    x_ref[b, b] = x22[...]
    x_ref[b, a] = -exact_nn(x22[...], exact_nn(l_in[b, :], x_in[...]))


def upper_nt(a, b):
    left = split_nt([v[:, :HALF] for v in a], [v[:HALF, :HALF] for v in b])
    right = split_nt(a, [v[HALF:, :] for v in b])
    return jnp.concatenate([left, right], axis=1)


def tangent_factor(x_ref, ad_ref, phi_ref):
    h = HALF
    x11, x21, x22 = x_ref[:h, :h], x_ref[h:, :h], x_ref[h:, h:]
    t11 = exact_nn(x11, ad_ref[:h, :h])
    t21 = exact_nn(x21, ad_ref[:h, :h]) + exact_nn(x22, ad_ref[h:, :h])
    t22 = exact_nn(x21, ad_ref[:h, h:]) + exact_nn(x22, ad_ref[h:, h:])
    ri = lax.broadcasted_iota(jnp.int32, (h, h), 0)
    ci = lax.broadcasted_iota(jnp.int32, (h, h), 1)
    weight = jnp.where(ri > ci, 1.0, jnp.where(ri == ci, 0.5, 0.0)).astype(F32)
    phi_ref[:h, :h] = exact_nt(t11, x11) * weight
    phi_ref[h:, :h] = exact_nt(t21, x11)
    phi_ref[h:, h:] = (exact_nt(t21, x21) + exact_nt(t22, x22)) * weight
    phi_ref[:h, h:] = jnp.zeros((h, h), F32)


def panel(*refs):
    at_ref, l_ref, x_ref = refs[:3]
    pieces = refs[3:11]
    parts, tangent_parts = refs[11:15], refs[15:19]
    strip_ref, strip_tangent_ref = refs[19:21]
    factor_out, change_out, panel_out, panel_change_out, strip_out, strip_change_out = refs[21:27]
    ad, raw, phi, xs, phis, qs, qds, rows_ref, done_ref = refs[27:]
    col = at_ref[1]
    whole = slice(None)

    @pl.when(pl.program_id(0) == 0)
    def _():
        spread(at_ref, pieces, (0,), ad)
        spread(at_ref, pieces, (1,), raw.at[0])
        spread(at_ref, pieces, (2,), raw.at[1])
        tangent_factor(x_ref, ad, phi)
        own = pl.ds(pl.multiple_of(at_ref[0] * 8, 8), 8)
        lanes = pl.ds(pl.multiple_of(col * 128, 128), 128)
        factor_out[...] = l_ref[own, lanes]
        change_out[...] = exact_nn(l_ref[own, :], phi[:, lanes])
        xs[0], xs[1] = halves(x_ref[...])
        phis[0], phis[1] = halves(phi[...])
        solved = upper_nt(halves(raw[...].reshape(2 * PIVOT, PIVOT)), [xs[0], xs[1]])
        q = halves(solved[:PIVOT])
        qs[0], qs[1] = q
        qds[0], qds[1] = halves(solved[PIVOT:] - upper_nt(q, [phis[0], phis[1]]))

    for shift, part, tangent_part in zip((0, 3, 1, 2), parts, tangent_parts):
        lanes = pl.ds(pl.multiple_of(lax.rem(col + shift, N_Y) * 128, 128), 128)
        for at, value in ((0, part[...]), (PANEL_TILE, tangent_part[...])):
            high, low = halves(value)
            rows_ref[0, at : at + PANEL_TILE, lanes] = high
            rows_ref[1, at : at + PANEL_TILE, lanes] = low
    solved = upper_nt([rows_ref[0], rows_ref[1]], [xs[0], xs[1]])
    factor = solved[:PANEL_TILE]
    factor_halves = halves(factor)
    change = solved[PANEL_TILE:] - upper_nt(factor_halves, [phis[0], phis[1]])
    change_halves = halves(change)
    done_ref[0] = factor
    done_ref[1] = change
    lanes = pl.ds(pl.multiple_of(col * 128, 128), 128)
    panel_out[...] = done_ref[0, :, lanes]
    panel_change_out[...] = done_ref[1, :, lanes]
    q = [qs[0], qs[1]]
    strip_out[...] = strip_ref[...] - split_nt(factor_halves, q)
    strip_change_out[...] = strip_tangent_ref[...] - (
        split_nt(change_halves, q) + split_nt(factor_halves, [qds[0], qds[1]])
    )


def row_index(x, z, core):
    return (x % N_X * N_Z + z % N_Z) * N_CORE + core % N_CORE


ALONG_Z = [
    [row_index(x, z, core) for z in range(N_Z)] for x in range(N_X) for core in range(N_CORE)
]

def along_y(value, s):
    return lax.ppermute(value, "col", [(c, (c + s) % N_Y) for c in range(N_Y)])


def along_x_core(value, s_x, s_core):
    pairs = [
        (row_index(x, z, core), row_index(x + s_x, z, core + s_core))
        for x in range(N_X)
        for z in range(N_Z)
        for core in range(N_CORE)
    ]
    return lax.ppermute(value, "row", pairs)


def gather_z(value):
    spread = jnp.broadcast_to(value[None], (N_Z,) + value.shape)
    return lax.all_to_all(spread, "row", 0, 0, axis_index_groups=ALONG_Z)


def body(pivot_block, pivot_tangent, panel_block, panel_tangent, strip_block, strip_tangent):
    row = lax.axis_index("row")
    col = lax.axis_index("col")
    at = jnp.stack([row, col, row // (N_Z * N_CORE), row % N_CORE]).astype(jnp.int32)

    def tiles(s):
        at_row = lax.rem(col + s, N_Y) * 8
        return jnp.stack(
            [
                pivot_block,
                pivot_tangent,
                lax.dynamic_slice_in_dim(panel_block, at_row, 8, 0),
                lax.dynamic_slice_in_dim(panel_tangent, at_row, 8, 0),
            ]
        )

    by_y = [tiles(0)] + [along_y(tiles(s), s) for s in range(1, N_Y)]
    gathered = gather_z(jnp.stack(by_y))
    pivot, rest = gathered[:, :, 0], gathered[:, :, 1:]
    pivot_pieces = [pivot] + [along_x_core(pivot, s, 0) for s in range(1, N_X)]
    pivot_pieces = pivot_pieces + [along_x_core(v, 0, 1) for v in pivot_pieces]
    own_core = [rest] + [along_x_core(rest, s, 0) for s in range(1, N_X)]
    rest_pieces = own_core + [along_x_core(v, 0, 1) for v in own_core]

    def around(value, forward_first):
        left, right = along_y(value, 1), along_y(value, 3)
        far = along_y(left, 1) if forward_first else along_y(right, 3)
        return [value, left, right, far]

    parts = around(panel_block, True)
    tangent_parts = around(panel_tangent, False)

    vmem = pl.BlockSpec(memory_space=pltpu.VMEM)
    smem = pl.BlockSpec(memory_space=pltpu.SMEM)

    def matrix(*shape):
        return jax.ShapeDtypeStruct(shape, F32)

    limit = pltpu.CompilerParams(vmem_limit_bytes=56 * 2**20)
    w22, l_left, x_first = pl.pallas_call(
        first_half,
        name="first_half",
        out_shape=(matrix(HALF, HALF), matrix(PIVOT, HALF), matrix(HALF, HALF)),
        in_specs=[smem] + [vmem] * 8,
        out_specs=[vmem] * 3,
        scratch_shapes=[pltpu.VMEM((PIVOT, PIVOT), F32)],
        compiler_params=limit,
        cost_estimate=pl.CostEstimate(flops=16 * 10**9, bytes_accessed=10**6, transcendentals=0),
    )(at, *pivot_pieces)
    whole_factor, inverse = pl.pallas_call(
        second_half,
        name="second_half",
        out_shape=(matrix(PIVOT, PIVOT), matrix(PIVOT, PIVOT)),
        in_specs=[vmem] * 3,
        out_specs=[vmem] * 2,
        scratch_shapes=[pltpu.VMEM((HALF, HALF), F32)] * 3,
        compiler_params=limit,
        cost_estimate=pl.CostEstimate(flops=16 * 10**9, bytes_accessed=10**6, transcendentals=0),
    )(w22, l_left, x_first)

    local_rows, local_strip = strip_block.shape
    tile = PANEL_TILE
    narrow = pl.BlockSpec((tile, 128), lambda i: (i, 0))
    broad = pl.BlockSpec((tile, local_strip), lambda i: (i, 0))
    corner = pl.BlockSpec((8, 128), lambda i: (0, 0))
    square = pltpu.VMEM((PIVOT, PIVOT), F32)
    split_square = pltpu.VMEM((2, PIVOT, PIVOT), BF16)
    return pl.pallas_call(
        panel,
        name="panel",
        grid=(local_rows // tile,),
        out_shape=(
            matrix(8, 128),
            matrix(8, 128),
            matrix(local_rows, 128),
            matrix(local_rows, 128),
            matrix(local_rows, local_strip),
            matrix(local_rows, local_strip),
        ),
        in_specs=[smem] + [vmem] * 10 + [narrow] * 8 + [broad] * 2,
        out_specs=(corner, corner, narrow, narrow, broad, broad),
        scratch_shapes=[
            square,
            pltpu.VMEM((2, PIVOT, PIVOT), F32),
            square,
            split_square,
            split_square,
            split_square,
            split_square,
            pltpu.VMEM((2, 2 * tile, PIVOT), BF16),
            pltpu.VMEM((2, tile, PIVOT), F32),
        ],
        compiler_params=limit,
        cost_estimate=pl.CostEstimate(flops=10**10, bytes_accessed=20 * 10**6, transcendentals=0),
    )(at, whole_factor, inverse, *rest_pieces, *parts, *tangent_parts, strip_block, strip_tangent)


def solution(mesh):
    spec = P("row", "col")
    return jax.shard_map(
        body, mesh=mesh, in_specs=(spec,) * 6, out_specs=(spec,) * 6, check_vma=False
    )
```

profile of v0, /device:TPU:1, one launch (start us, length us, event | category | flops | bytes accessed | tf_op | source)
XLA Modules:
  0.0 113.2 jit_solution(18373499628978216394)
XLA Ops:
  0.6 0.0 copy-start.2
  0.7 0.8 dynamic-slice_bitcast_fusion.7
  1.5 0.7 dynamic-slice_bitcast_fusion.6
  2.2 0.7 maximum_bitcast_fusion
  2.9 2.1 %collective-permute-start = (f32[4,8,128]{2,1,0:T(8,128)S(1)}, f32[4,8,128]{2,1,0:T(8,128)S(1)}, u32[]{:S(2)}, u32[]{:S(2)}) collective-permute-start(f32[4,8,128]{2,1,0:T(8,128)S(1)} %get-tuple-element.25), channel_id=1, source_target_pairs={{0,1},{1,2},{2,3},{3,0},{4,5},{5,6},{6,7},{7,4},{8,9},{9,10},{10,1... | collective-permute-start | bytes 49160 | tf_op jit(solution)/shard_map/ppermute | solution.py:268
  5.0 2.6 %collective-permute-start.1 = (f32[4,8,128]{2,1,0:T(8,128)S(1)}, f32[4,8,128]{2,1,0:T(8,128)S(1)}, u32[]{:S(2)}, u32[]{:S(2)}) collective-permute-start(f32[4,8,128]{2,1,0:T(8,128)S(1)} %get-tuple-element.26), channel_id=1, source_target_pairs={{0,2},{1,3},{2,0},{3,1},{4,6},{5,7},{6,4},{7,5},{8,10},{9,11},{10,... | collective-permute-start | bytes 49160 | tf_op jit(solution)/shard_map/ppermute | solution.py:268
  7.7 1.1 collective-permute-start.2
  8.7 0.4 collective-permute-done.1
  9.1 1.4 %collective-permute-done.2 = f32[4,8,128]{2,1,0:T(8,128)S(1)} collective-permute-done((f32[4,8,128]{2,1,0:T(8,128)S(1)}, f32[4,8,128]{2,1,0:T(8,128)S(1)}, u32[]{:S(2)}, u32[]{:S(2)}) %collective-permute-start.2) | collective-permute-done | bytes 16416 | tf_op jit(solution)/shard_map/ppermute | solution.py:268
  10.6 0.9 broadcast_in_dim.2
  11.4 8.2 %all-to-all-start = ((f32[8,4,4,8,128]{4,3,2,1,0:T(8,128)}), f32[8,4,4,8,128]{4,3,2,1,0:T(8,128)S(1)}, u32[]{:S(2)}, u32[]{:S(2)}) async-start(f32[8,4,4,8,128]{4,3,2,1,0:T(8,128)} %broadcast_in_dim.2), calls=%async_computation | async-start | bytes 1048576 | tf_op jit(solution)/shard_map/all_to_all | solution.py:283
  19.6 0.0 collective-permute-start.17
  19.6 2.7 %collective-permute-start.18 = (f32[1024,128]{1,0:T(8,128)}, f32[1024,128]{1,0:T(8,128)S(1)}, u32[]{:S(2)}, u32[]{:S(2)}) collective-permute-start(f32[1024,128]{1,0:T(8,128)} %refs_11_.1), channel_id=1, source_target_pairs={{0,3},{1,0},{2,1},{3,2},{4,7},{5,4},{6,5},{7,6},{8,11},{9,8},{10,9... | collective-permute-start | bytes 1572872 | tf_op jit(solution)/shard_map/ppermute | solution.py:268
  22.3 12.4 %all-to-all-done = f32[8,4,4,8,128]{4,3,2,1,0:T(8,128)S(1)} async-done(((f32[8,4,4,8,128]{4,3,2,1,0:T(8,128)}), f32[8,4,4,8,128]{4,3,2,1,0:T(8,128)S(1)}, u32[]{:S(2)}, u32[]{:S(2)}) %all-to-all-start) | async-done | bytes 524320 | tf_op jit(solution)/shard_map/all_to_all | solution.py:283
  34.7 0.0 copy-start.1
  34.8 2.6 %collective-permute-start.5 = (f32[8,4,8,128]{3,2,1,0:T(8,128)S(1)}, f32[8,4,8,128]{3,2,1,0:T(8,128)S(1)}, u32[]{:S(2)}, u32[]{:S(2)}) collective-permute-start(f32[8,4,8,128]{3,2,1,0:T(8,128)S(1)} %slice_bitcast_fusion.refs_1_), channel_id=1, source_target_pairs={{0,192},{4,196},{8,200},{12,204},{16,208},{20,212},{24,216},{28,22... | collective-permute-start | bytes 393224 | tf_op jit(solution)/shard_map/ppermute | solution.py:278
  37.3 0.5 collective-permute-start.4
  37.8 0.0 collective-permute-done.17.refs_12_
  37.8 0.6 collective-permute-start.3
  38.4 0.0 collective-permute-done.18.refs_13_
  38.4 4.2 %collective-permute-start.6 = (f32[8,4,8,128]{3,2,1,0:T(8,128)S(1)}, f32[8,4,8,128]{3,2,1,0:T(8,128)S(1)}, u32[]{:S(2)}, u32[]{:S(2)}) collective-permute-start(f32[8,4,8,128]{3,2,1,0:T(8,128)S(1)} %slice_bitcast_fusion.refs_1_), channel_id=1, source_target_pairs={{0,4},{4,0},{8,12},{12,8},{16,20},{20,16},{24,28},{28,24},{32,36},... | collective-permute-start | bytes 393224 | tf_op jit(solution)/shard_map/ppermute | solution.py:278
  42.6 0.0 collective-permute-done.5.refs_4_
  42.6 2.2 %collective-permute-start.9 = (f32[8,4,8,128]{3,2,1,0:T(8,128)S(1)}, f32[8,4,8,128]{3,2,1,0:T(8,128)S(1)}, u32[]{:S(2)}, u32[]{:S(2)}) collective-permute-start(f32[8,4,8,128]{3,2,1,0:T(8,128)S(1)} %collective-permute-done.5.refs_4_), channel_id=1, source_target_pairs={{0,4},{4,0},{8,12},{12,8},{16,20},{20,16},{24,28},{28,24},{32,36},... | collective-permute-start | bytes 393224 | tf_op jit(solution)/shard_map/ppermute | solution.py:278
  44.8 0.0 collective-permute-done.4.refs_3_
  44.8 2.6 %collective-permute-start.8 = (f32[8,4,8,128]{3,2,1,0:T(8,128)S(1)}, f32[8,4,8,128]{3,2,1,0:T(8,128)S(1)}, u32[]{:S(2)}, u32[]{:S(2)}) collective-permute-start(f32[8,4,8,128]{3,2,1,0:T(8,128)S(1)} %collective-permute-done.4.refs_3_), channel_id=1, source_target_pairs={{0,4},{4,0},{8,12},{12,8},{16,20},{20,16},{24,28},{28,24},{32,36},... | collective-permute-start | bytes 393224 | tf_op jit(solution)/shard_map/ppermute | solution.py:278
  47.5 1.3 %collective-permute-start.7 = (f32[8,4,8,128]{3,2,1,0:T(8,128)S(1)}, f32[8,4,8,128]{3,2,1,0:T(8,128)}, u32[]{:S(2)}, u32[]{:S(2)}) collective-permute-start(f32[8,4,8,128]{3,2,1,0:T(8,128)S(1)} %collective-permute-done.3.refs_2_), channel_id=1, source_target_pairs={{0,4},{4,0},{8,12},{12,8},{16,20},{20,16},{24,28},{28,24},{32,36},... | collective-permute-start | bytes 393224 | tf_op jit(solution)/shard_map/ppermute | solution.py:278
  48.8 0.6 pad_add_fusion.refs_0_
  49.5 2.1 %collective-permute-start.21 = (f32[1024,128]{1,0:T(8,128)S(1)}, f32[1024,128]{1,0:T(8,128)S(1)}, u32[]{:S(2)}, u32[]{:S(2)}) collective-permute-start(f32[1024,128]{1,0:T(8,128)S(1)} %copy-done.2), channel_id=1, source_target_pairs={{0,3},{1,0},{2,1},{3,2},{4,7},{5,4},{6,5},{7,6},{8,11},{9,8},{10,9... | collective-permute-start | bytes 1572872 | tf_op jit(solution)/shard_map/ppermute | solution.py:268
  51.5 0.0 collective-permute-done.6.refs_5_
  51.5 0.0 collective-permute-done.9.refs_8_
  51.5 0.4 collective-permute-start.12
  51.9 0.0 collective-permute-done.8.refs_7_
  51.9 0.5 collective-permute-start.11
  52.4 0.9 collective-permute-start.10
  53.4 14.2 %first_half.1 = (f32[256,256]{1,0:T(8,128)}, f32[512,256]{1,0:T(8,128)}, f32[256,256]{1,0:T(8,128)}) custom-call(s32[4]{0:T(128)} %pad_add_fusion.refs_0_, f32[8,4,8,128]{3,2,1,0:T(8,128)} %copy-done.1, f32[8,4,8,128]{3,2,1,0:T(8,128)} %copy-done.18, f32[8,4,8,128]{3,2,1,0:T(8,128)} %copy-done.17, f32[8,4,8,128]{3,2,1,0:T(8,128)} %copy-done.16, ...), custom_call_target="tpu_custom_call" | custom-call | flops 16000000000 | bytes 1000000 | tf_op jit(solution)/shard_map/first_half/pallas_call | solution.py:325
  67.7 2.7 %collective-permute-start.22 = (f32[1024,128]{1,0:T(8,128)S(1)}, f32[1024,128]{1,0:T(8,128)S(1)}, u32[]{:S(2)}, u32[]{:S(2)}) collective-permute-start(f32[1024,128]{1,0:T(8,128)S(1)} %collective-permute-done.21.refs_17_), channel_id=1, source_target_pairs={{0,3},{1,0},{2,1},{3,2},{4,7},{5,4},{6,5},{7,6},{8,11},{9,8},{10,9... | collective-permute-start | bytes 1572872 | tf_op jit(solution)/shard_map/ppermute | solution.py:268
  70.3 1.5 %collective-permute-start.13 = (f32[8,4,3,8,128]{4,3,2,1,0:T(8,128)S(1)}, f32[8,4,3,8,128]{4,3,2,1,0:T(8,128)S(1)}, u32[]{:S(2)}, u32[]{:S(2)}) collective-permute-start(f32[8,4,3,8,128]{4,3,2,1,0:T(8,128)S(1)} %slice.9.refs_3_), channel_id=1, source_target_pairs={{0,4},{4,0},{8,12},{12,8},{16,20},{20,16},{24,28},{28,24},{32,36},... | collective-permute-start | bytes 1179656 | tf_op jit(solution)/shard_map/ppermute | solution.py:278
  71.8 0.1 collective-permute-start.16
  72.0 0.4 collective-permute-start.15
  72.4 0.5 collective-permute-done.10.refs_4_
  72.9 0.5 collective-permute-start.14
  73.4 14.3 %second_half.1 = (f32[512,512]{1,0:T(8,128)}, f32[512,512]{1,0:T(8,128)}) custom-call(f32[256,256]{1,0:T(8,128)} %get-tuple-element.11.w_in, f32[512,256]{1,0:T(8,128)} %get-tuple-element.12.l_in, f32[256,256]{1,0:T(8,128)} %get-tuple-element.13.x_in), custom_call_target="tpu_custom_call" | custom-call | flops 16000000000 | bytes 1000000 | tf_op jit(solution)/shard_map/second_half/pallas_call | solution.py:335
  87.8 0.7 copy-done.8
  88.5 0.1 copy-done.12
  88.6 0.1 copy-done.13
  88.8 0.1 copy-done.14
  88.9 0.2 copy-done.15
  89.1 23.9 %panel.1 = (f32[8,128]{1,0:T(8,128)}, f32[8,128]{1,0:T(8,128)}, f32[1024,128]{1,0:T(8,128)}, f32[1024,128]{1,0:T(8,128)}, f32[1024,512]{1,0:T(8,128)}, /*index=5*/f32[1024,512]{1,0:T(8,128)}) custom-call(s32[4]{0:T(128)} %pad_add_fusion.refs_0_, f32[512,512]{1,0:T(8,128)} %get-tuple-element.14.refs_1_, f32[512,512]{1,0:T(8,128)} %get-tuple-element.15.refs_2_, ...), custom_call_target="tpu_custom_call" | custom-call | flops 10000000000 | bytes 20000000 | tf_op jit(solution)/shard_map/panel/pallas_call | solution.py:353
  (55 shorter events, 0.2 us)
Async XLA Ops:
  0.6 48.8 %copy-start.2 = (f32[1024,128]{1,0:T(8,128)S(1)}, f32[1024,128]{1,0:T(8,128)}, u32[]{:S(2)}) copy-start(f32[1024,128]{1,0:T(8,128)} %refs_15_.1) | copy-start | bytes 1572868
  2.9 5.8 %collective-permute-start = (f32[4,8,128]{2,1,0:T(8,128)S(1)}, f32[4,8,128]{2,1,0:T(8,128)S(1)}, u32[]{:S(2)}, u32[]{:S(2)}) collective-permute-start(f32[4,8,128]{2,1,0:T(8,128)S(1)} %get-tuple-element.25), channel_id=1, source_target_pairs={{0,1},{1,2},{2,3},{3,0},{4,5},{5,6},{6,7},{7,4},{8,9},{9,10},{10,1... | collective-permute-start | bytes 49160 | tf_op jit(solution)/shard_map/ppermute | solution.py:268
  5.0 4.1 %collective-permute-start.1 = (f32[4,8,128]{2,1,0:T(8,128)S(1)}, f32[4,8,128]{2,1,0:T(8,128)S(1)}, u32[]{:S(2)}, u32[]{:S(2)}) collective-permute-start(f32[4,8,128]{2,1,0:T(8,128)S(1)} %get-tuple-element.26), channel_id=1, source_target_pairs={{0,2},{1,3},{2,0},{3,1},{4,6},{5,7},{6,4},{7,5},{8,10},{9,11},{10,... | collective-permute-start | bytes 49160 | tf_op jit(solution)/shard_map/ppermute | solution.py:268
  7.7 2.9 %collective-permute-start.2 = (f32[4,8,128]{2,1,0:T(8,128)S(1)}, f32[4,8,128]{2,1,0:T(8,128)S(1)}, u32[]{:S(2)}, u32[]{:S(2)}) collective-permute-start(f32[4,8,128]{2,1,0:T(8,128)S(1)} %get-tuple-element.27), channel_id=1, source_target_pairs={{0,3},{1,0},{2,1},{3,2},{4,7},{5,4},{6,5},{7,6},{8,11},{9,8},{10,9... | collective-permute-start | bytes 49160 | tf_op jit(solution)/shard_map/ppermute | solution.py:268
  11.4 23.3 %all-to-all-start = ((f32[8,4,4,8,128]{4,3,2,1,0:T(8,128)}), f32[8,4,4,8,128]{4,3,2,1,0:T(8,128)S(1)}, u32[]{:S(2)}, u32[]{:S(2)}) async-start(f32[8,4,4,8,128]{4,3,2,1,0:T(8,128)} %broadcast_in_dim.2), calls=%async_computation | async-start | bytes 1048576 | tf_op jit(solution)/shard_map/all_to_all | solution.py:283
  19.6 18.2 %collective-permute-start.17 = (f32[1024,128]{1,0:T(8,128)}, f32[1024,128]{1,0:T(8,128)S(1)}, u32[]{:S(2)}, u32[]{:S(2)}) collective-permute-start(f32[1024,128]{1,0:T(8,128)} %refs_11_.1), channel_id=1, source_target_pairs={{0,1},{1,2},{2,3},{3,0},{4,5},{5,6},{6,7},{7,4},{8,9},{9,10},{10,1... | collective-permute-start | bytes 1572872 | tf_op jit(solution)/shard_map/ppermute | solution.py:268
  19.6 18.8 %collective-permute-start.18 = (f32[1024,128]{1,0:T(8,128)}, f32[1024,128]{1,0:T(8,128)S(1)}, u32[]{:S(2)}, u32[]{:S(2)}) collective-permute-start(f32[1024,128]{1,0:T(8,128)} %refs_11_.1), channel_id=1, source_target_pairs={{0,3},{1,0},{2,1},{3,2},{4,7},{5,4},{6,5},{7,6},{8,11},{9,8},{10,9... | collective-permute-start | bytes 1572872 | tf_op jit(solution)/shard_map/ppermute | solution.py:268
  22.3 27.2 %collective-permute-start.20 = (f32[1024,128]{1,0:T(8,128)}, f32[1024,128]{1,0:T(8,128)S(1)}, u32[]{:S(2)}, u32[]{:S(2)}) collective-permute-start(f32[1024,128]{1,0:T(8,128)} %refs_15_.1), channel_id=1, source_target_pairs={{0,1},{1,2},{2,3},{3,0},{4,5},{5,6},{6,7},{7,4},{8,9},{9,10},{10,1... | collective-permute-start | bytes 1572872 | tf_op jit(solution)/shard_map/ppermute | solution.py:268
  34.7 18.6 %copy-start.1 = (f32[8,4,8,128]{3,2,1,0:T(8,128)}, f32[8,4,8,128]{3,2,1,0:T(8,128)S(1)}, u32[]{:S(2)}) copy-start(f32[8,4,8,128]{3,2,1,0:T(8,128)S(1)} %slice_bitcast_fusion.refs_1_) | copy-start | bytes 393220
  34.8 7.9 %collective-permute-start.5 = (f32[8,4,8,128]{3,2,1,0:T(8,128)S(1)}, f32[8,4,8,128]{3,2,1,0:T(8,128)S(1)}, u32[]{:S(2)}, u32[]{:S(2)}) collective-permute-start(f32[8,4,8,128]{3,2,1,0:T(8,128)S(1)} %slice_bitcast_fusion.refs_1_), channel_id=1, source_target_pairs={{0,192},{4,196},{8,200},{12,204},{16,208},{20,212},{24,216},{28,22... | collective-permute-start | bytes 393224 | tf_op jit(solution)/shard_map/ppermute | solution.py:278
  37.3 7.5 %collective-permute-start.4 = (f32[8,4,8,128]{3,2,1,0:T(8,128)S(1)}, f32[8,4,8,128]{3,2,1,0:T(8,128)S(1)}, u32[]{:S(2)}, u32[]{:S(2)}) collective-permute-start(f32[8,4,8,128]{3,2,1,0:T(8,128)S(1)} %slice_bitcast_fusion.refs_1_), channel_id=1, source_target_pairs={{0,128},{4,132},{8,136},{12,140},{16,144},{20,148},{24,152},{28,15... | collective-permute-start | bytes 393224 | tf_op jit(solution)/shard_map/ppermute | solution.py:278
  37.8 29.8 %copy-start.3 = (f32[1024,128]{1,0:T(8,128)}, f32[1024,128]{1,0:T(8,128)S(1)}, u32[]{:S(2)}) copy-start(f32[1024,128]{1,0:T(8,128)S(1)} %collective-permute-done.17.refs_12_) | copy-start | bytes 1572868
  37.8 9.7 %collective-permute-start.3 = (f32[8,4,8,128]{3,2,1,0:T(8,128)S(1)}, f32[8,4,8,128]{3,2,1,0:T(8,128)S(1)}, u32[]{:S(2)}, u32[]{:S(2)}) collective-permute-start(f32[8,4,8,128]{3,2,1,0:T(8,128)S(1)} %slice_bitcast_fusion.refs_1_), channel_id=1, source_target_pairs={{0,64},{4,68},{8,72},{12,76},{16,80},{20,84},{24,88},{28,92},{32,9... | collective-permute-start | bytes 393224 | tf_op jit(solution)/shard_map/ppermute | solution.py:278
  38.4 29.2 %copy-start.4 = (f32[1024,128]{1,0:T(8,128)}, f32[1024,128]{1,0:T(8,128)S(1)}, u32[]{:S(2)}) copy-start(f32[1024,128]{1,0:T(8,128)S(1)} %collective-permute-done.18.refs_13_) | copy-start | bytes 1572868
  38.4 13.1 %collective-permute-start.6 = (f32[8,4,8,128]{3,2,1,0:T(8,128)S(1)}, f32[8,4,8,128]{3,2,1,0:T(8,128)S(1)}, u32[]{:S(2)}, u32[]{:S(2)}) collective-permute-start(f32[8,4,8,128]{3,2,1,0:T(8,128)S(1)} %slice_bitcast_fusion.refs_1_), channel_id=1, source_target_pairs={{0,4},{4,0},{8,12},{12,8},{16,20},{20,16},{24,28},{28,24},{32,36},... | collective-permute-start | bytes 393224 | tf_op jit(solution)/shard_map/ppermute | solution.py:278
  42.6 10.8 %copy-start.16 = (f32[8,4,8,128]{3,2,1,0:T(8,128)}, f32[8,4,8,128]{3,2,1,0:T(8,128)S(1)}, u32[]{:S(2)}) copy-start(f32[8,4,8,128]{3,2,1,0:T(8,128)S(1)} %collective-permute-done.5.refs_4_) | copy-start | bytes 393220
  42.6 8.9 %collective-permute-start.9 = (f32[8,4,8,128]{3,2,1,0:T(8,128)S(1)}, f32[8,4,8,128]{3,2,1,0:T(8,128)S(1)}, u32[]{:S(2)}, u32[]{:S(2)}) collective-permute-start(f32[8,4,8,128]{3,2,1,0:T(8,128)S(1)} %collective-permute-done.5.refs_4_), channel_id=1, source_target_pairs={{0,4},{4,0},{8,12},{12,8},{16,20},{20,16},{24,28},{28,24},{32,36},... | collective-permute-start | bytes 393224 | tf_op jit(solution)/shard_map/ppermute | solution.py:278
  44.8 8.5 %copy-start.17 = (f32[8,4,8,128]{3,2,1,0:T(8,128)}, f32[8,4,8,128]{3,2,1,0:T(8,128)S(1)}, u32[]{:S(2)}) copy-start(f32[8,4,8,128]{3,2,1,0:T(8,128)S(1)} %collective-permute-done.4.refs_3_) | copy-start | bytes 393220
  44.8 7.1 %collective-permute-start.8 = (f32[8,4,8,128]{3,2,1,0:T(8,128)S(1)}, f32[8,4,8,128]{3,2,1,0:T(8,128)S(1)}, u32[]{:S(2)}, u32[]{:S(2)}) collective-permute-start(f32[8,4,8,128]{3,2,1,0:T(8,128)S(1)} %collective-permute-done.4.refs_3_), channel_id=1, source_target_pairs={{0,4},{4,0},{8,12},{12,8},{16,20},{20,16},{24,28},{28,24},{32,36},... | collective-permute-start | bytes 393224 | tf_op jit(solution)/shard_map/ppermute | solution.py:278
  47.5 5.9 %copy-start.18 = (f32[8,4,8,128]{3,2,1,0:T(8,128)}, f32[8,4,8,128]{3,2,1,0:T(8,128)S(1)}, u32[]{:S(2)}) copy-start(f32[8,4,8,128]{3,2,1,0:T(8,128)S(1)} %collective-permute-done.3.refs_2_) | copy-start | bytes 393220
  47.5 4.9 %collective-permute-start.7 = (f32[8,4,8,128]{3,2,1,0:T(8,128)S(1)}, f32[8,4,8,128]{3,2,1,0:T(8,128)}, u32[]{:S(2)}, u32[]{:S(2)}) collective-permute-start(f32[8,4,8,128]{3,2,1,0:T(8,128)S(1)} %collective-permute-done.3.refs_2_), channel_id=1, source_target_pairs={{0,4},{4,0},{8,12},{12,8},{16,20},{20,16},{24,28},{28,24},{32,36},... | collective-permute-start | bytes 393224 | tf_op jit(solution)/shard_map/ppermute | solution.py:278
  49.4 20.9 %copy-start = (f32[8,4,3,8,128]{4,3,2,1,0:T(8,128)}, f32[8,4,3,8,128]{4,3,2,1,0:T(8,128)S(1)}, u32[]{:S(2)}) copy-start(f32[8,4,3,8,128]{4,3,2,1,0:T(8,128)S(1)} %slice.9.refs_3_) | copy-start | bytes 1179652
  49.4 18.2 %copy-start.5 = (f32[1024,128]{1,0:T(8,128)}, f32[1024,128]{1,0:T(8,128)S(1)}, u32[]{:S(2)}) copy-start(f32[1024,128]{1,0:T(8,128)S(1)} %collective-permute-done.20.refs_16_) | copy-start | bytes 1572868
  49.5 18.2 %collective-permute-start.21 = (f32[1024,128]{1,0:T(8,128)S(1)}, f32[1024,128]{1,0:T(8,128)S(1)}, u32[]{:S(2)}, u32[]{:S(2)}) collective-permute-start(f32[1024,128]{1,0:T(8,128)S(1)} %copy-done.2), channel_id=1, source_target_pairs={{0,3},{1,0},{2,1},{3,2},{4,7},{5,4},{6,5},{7,6},{8,11},{9,8},{10,9... | collective-permute-start | bytes 1572872 | tf_op jit(solution)/shard_map/ppermute | solution.py:268
  51.5 1.9 %copy-start.19 = (f32[8,4,8,128]{3,2,1,0:T(8,128)}, f32[8,4,8,128]{3,2,1,0:T(8,128)S(1)}, u32[]{:S(2)}) copy-start(f32[8,4,8,128]{3,2,1,0:T(8,128)S(1)} %collective-permute-done.6.refs_5_) | copy-start | bytes 393220
  51.5 18.8 %collective-permute-start.19 = (f32[1024,128]{1,0:T(8,128)S(1)}, f32[1024,128]{1,0:T(8,128)S(1)}, u32[]{:S(2)}, u32[]{:S(2)}) collective-permute-start(f32[1024,128]{1,0:T(8,128)S(1)} %collective-permute-done.17.refs_12_), channel_id=1, source_target_pairs={{0,1},{1,2},{2,3},{3,0},{4,5},{5,6},{6,7},{7,4},{8,9},{9,10},{10,1... | collective-permute-start | bytes 1572872 | tf_op jit(solution)/shard_map/ppermute | solution.py:268
  51.5 1.9 %copy-start.20 = (f32[8,4,8,128]{3,2,1,0:T(8,128)}, f32[8,4,8,128]{3,2,1,0:T(8,128)S(1)}, u32[]{:S(2)}) copy-start(f32[8,4,8,128]{3,2,1,0:T(8,128)S(1)} %collective-permute-done.9.refs_8_) | copy-start | bytes 393220
  51.5 20.3 %collective-permute-start.12 = (f32[8,4,3,8,128]{4,3,2,1,0:T(8,128)S(1)}, f32[8,4,3,8,128]{4,3,2,1,0:T(8,128)S(1)}, u32[]{:S(2)}, u32[]{:S(2)}) collective-permute-start(f32[8,4,3,8,128]{4,3,2,1,0:T(8,128)S(1)} %slice.9.refs_3_), channel_id=1, source_target_pairs={{0,192},{4,196},{8,200},{12,204},{16,208},{20,212},{24,216},{28,22... | collective-permute-start | bytes 1179656 | tf_op jit(solution)/shard_map/ppermute | solution.py:278
  51.9 1.5 %copy-start.21 = (f32[8,4,8,128]{3,2,1,0:T(8,128)}, f32[8,4,8,128]{3,2,1,0:T(8,128)S(1)}, u32[]{:S(2)}) copy-start(f32[8,4,8,128]{3,2,1,0:T(8,128)S(1)} %collective-permute-done.8.refs_7_) | copy-start | bytes 393220
  51.9 20.0 %collective-permute-start.11 = (f32[8,4,3,8,128]{4,3,2,1,0:T(8,128)S(1)}, f32[8,4,3,8,128]{4,3,2,1,0:T(8,128)S(1)}, u32[]{:S(2)}, u32[]{:S(2)}) collective-permute-start(f32[8,4,3,8,128]{4,3,2,1,0:T(8,128)S(1)} %slice.9.refs_3_), channel_id=1, source_target_pairs={{0,128},{4,132},{8,136},{12,140},{16,144},{20,148},{24,152},{28,15... | collective-permute-start | bytes 1179656 | tf_op jit(solution)/shard_map/ppermute | solution.py:278
  52.4 20.4 %collective-permute-start.10 = (f32[8,4,3,8,128]{4,3,2,1,0:T(8,128)S(1)}, f32[8,4,3,8,128]{4,3,2,1,0:T(8,128)S(1)}, u32[]{:S(2)}, u32[]{:S(2)}) collective-permute-start(f32[8,4,3,8,128]{4,3,2,1,0:T(8,128)S(1)} %slice.9.refs_3_), channel_id=1, source_target_pairs={{0,64},{4,68},{8,72},{12,76},{16,80},{20,84},{24,88},{28,92},{32,9... | collective-permute-start | bytes 1179656 | tf_op jit(solution)/shard_map/ppermute | solution.py:278
  67.7 20.0 %copy-start.6 = (f32[1024,128]{1,0:T(8,128)}, f32[1024,128]{1,0:T(8,128)S(1)}, u32[]{:S(2)}) copy-start(f32[1024,128]{1,0:T(8,128)S(1)} %collective-permute-done.21.refs_17_) | copy-start | bytes 1572868
  67.7 20.0 %collective-permute-start.22 = (f32[1024,128]{1,0:T(8,128)S(1)}, f32[1024,128]{1,0:T(8,128)S(1)}, u32[]{:S(2)}, u32[]{:S(2)}) collective-permute-start(f32[1024,128]{1,0:T(8,128)S(1)} %collective-permute-done.21.refs_17_), channel_id=1, source_target_pairs={{0,3},{1,0},{2,1},{3,2},{4,7},{5,4},{6,5},{7,6},{8,11},{9,8},{10,9... | collective-permute-start | bytes 1572872 | tf_op jit(solution)/shard_map/ppermute | solution.py:268
  70.3 17.3 %copy-start.7 = (f32[1024,128]{1,0:T(8,128)}, f32[1024,128]{1,0:T(8,128)S(1)}, u32[]{:S(2)}) copy-start(f32[1024,128]{1,0:T(8,128)S(1)} %collective-permute-done.19.refs_14_) | copy-start | bytes 1572868
  70.3 17.4 %collective-permute-start.13 = (f32[8,4,3,8,128]{4,3,2,1,0:T(8,128)S(1)}, f32[8,4,3,8,128]{4,3,2,1,0:T(8,128)S(1)}, u32[]{:S(2)}, u32[]{:S(2)}) collective-permute-start(f32[8,4,3,8,128]{4,3,2,1,0:T(8,128)S(1)} %slice.9.refs_3_), channel_id=1, source_target_pairs={{0,4},{4,0},{8,12},{12,8},{16,20},{20,16},{24,28},{28,24},{32,36},... | collective-permute-start | bytes 1179656 | tf_op jit(solution)/shard_map/ppermute | solution.py:278
  71.8 15.8 %copy-start.9 = (f32[8,4,3,8,128]{4,3,2,1,0:T(8,128)}, f32[8,4,3,8,128]{4,3,2,1,0:T(8,128)S(1)}, u32[]{:S(2)}) copy-start(f32[8,4,3,8,128]{4,3,2,1,0:T(8,128)S(1)} %collective-permute-done.12.refs_6_) | copy-start | bytes 1179652
  71.8 15.9 %collective-permute-start.16 = (f32[8,4,3,8,128]{4,3,2,1,0:T(8,128)S(1)}, f32[8,4,3,8,128]{4,3,2,1,0:T(8,128)S(1)}, u32[]{:S(2)}, u32[]{:S(2)}) collective-permute-start(f32[8,4,3,8,128]{4,3,2,1,0:T(8,128)S(1)} %collective-permute-done.12.refs_6_), channel_id=1, source_target_pairs={{0,4},{4,0},{8,12},{12,8},{16,20},{20,16},{24,28},{28,24},{32,36},... | collective-permute-start | bytes 1179656 | tf_op jit(solution)/shard_map/ppermute | solution.py:278
  72.0 15.7 %copy-start.10 = (f32[8,4,3,8,128]{4,3,2,1,0:T(8,128)}, f32[8,4,3,8,128]{4,3,2,1,0:T(8,128)S(1)}, u32[]{:S(2)}) copy-start(f32[8,4,3,8,128]{4,3,2,1,0:T(8,128)S(1)} %collective-permute-done.11.refs_5_) | copy-start | bytes 1179652
  72.0 15.8 %collective-permute-start.15 = (f32[8,4,3,8,128]{4,3,2,1,0:T(8,128)S(1)}, f32[8,4,3,8,128]{4,3,2,1,0:T(8,128)S(1)}, u32[]{:S(2)}, u32[]{:S(2)}) collective-permute-start(f32[8,4,3,8,128]{4,3,2,1,0:T(8,128)S(1)} %collective-permute-done.11.refs_5_), channel_id=1, source_target_pairs={{0,4},{4,0},{8,12},{12,8},{16,20},{20,16},{24,28},{28,24},{32,36},... | collective-permute-start | bytes 1179656 | tf_op jit(solution)/shard_map/ppermute | solution.py:278
  72.9 14.8 %copy-start.11 = (f32[8,4,3,8,128]{4,3,2,1,0:T(8,128)}, f32[8,4,3,8,128]{4,3,2,1,0:T(8,128)S(1)}, u32[]{:S(2)}) copy-start(f32[8,4,3,8,128]{4,3,2,1,0:T(8,128)S(1)} %collective-permute-done.10.refs_4_) | copy-start | bytes 1179652
  72.9 14.9 %collective-permute-start.14 = (f32[8,4,3,8,128]{4,3,2,1,0:T(8,128)S(1)}, f32[8,4,3,8,128]{4,3,2,1,0:T(8,128)S(1)}, u32[]{:S(2)}, u32[]{:S(2)}) collective-permute-start(f32[8,4,3,8,128]{4,3,2,1,0:T(8,128)S(1)} %collective-permute-done.10.refs_4_), channel_id=1, source_target_pairs={{0,4},{4,0},{8,12},{12,8},{16,20},{20,16},{24,28},{28,24},{32,36},... | collective-permute-start | bytes 1179656 | tf_op jit(solution)/shard_map/ppermute | solution.py:278
  87.7 0.8 copy-start.8
  87.7 0.9 copy-start.12
  87.8 1.0 copy-start.13
  87.8 1.2 %copy-start.14 = (f32[8,4,3,8,128]{4,3,2,1,0:T(8,128)}, f32[8,4,3,8,128]{4,3,2,1,0:T(8,128)S(1)}, u32[]{:S(2)}) copy-start(f32[8,4,3,8,128]{4,3,2,1,0:T(8,128)S(1)} %collective-permute-done.15.refs_9_) | copy-start | bytes 1179652
  87.8 1.3 %copy-start.15 = (f32[8,4,3,8,128]{4,3,2,1,0:T(8,128)}, f32[8,4,3,8,128]{4,3,2,1,0:T(8,128)S(1)}, u32[]{:S(2)}) copy-start(f32[8,4,3,8,128]{4,3,2,1,0:T(8,128)S(1)} %collective-permute-done.14.refs_8_) | copy-start | bytes 1179652
where the time goes:
time: 113 us
  Pallas kernels  52.4 us (46%)
  starting transfers between devices  39.7 us (35%)
  waiting for transfers between devices  14.8 us (13%)
  local copies, waits for them, and re-layouts  3.82 us (3%)
  other arithmetic  1.29 us (1%)
    pallas_call x1, Pallas kernels, body(): pl.pallas_call(panel, name='panel', grid=(local_rows // tile,), out_shape...  23.9 us
    ppermute x14, starting transfers between devices, along_x_core(): return lax.ppermute(value, 'row', pairs)  18.3 us
    pallas_call x1, Pallas kernels, body(): pl.pallas_call(second_half, name='second_half', out_shape=(matrix(PIVOT,...  14.3 us
    pallas_call x1, Pallas kernels, body(): pl.pallas_call(first_half, name='first_half', out_shape=(matrix(HALF, HAL...  14.2 us
    ppermute x9, starting transfers between devices, along_y(): return lax.ppermute(value, 'col', [(c, (c + s) % N_Y) for c in range(N_Y)])  13.2 us
    all_to_all x1, waiting for transfers between devices, gather_z(): return lax.all_to_all(spread, 'row', 0, 0, axis_index_groups=ALONG_Z)  12.4 us
    all_to_all x1, starting transfers between devices, gather_z(): return lax.all_to_all(spread, 'row', 0, 0, axis_index_groups=ALONG_Z)  8.19 us
  transfers between devices with their start and end apart: 24, of which 4 were waited for; matrix products, arithmetic and copies ran while one was open for 1% of the time, Pallas kernels for 25%

commit v1 on v0

v1 whole, which is shorter than its diff:
```python
import jax
import jax.numpy as jnp
from jax import lax
from jax.experimental import pallas as pl
from jax.experimental.pallas import tpu as pltpu
from jax.sharding import PartitionSpec as P

PIVOT = 512
HALF = PIVOT // 2
BLOCK = 128
GROUPS = BLOCK // 8
PANEL_TILE = 256
F32 = jnp.float32
BF16 = jnp.bfloat16
N_X, N_Z, N_CORE, N_Y = 4, 8, 2, 4


def thirds(x):
    first = x.astype(BF16)
    rest = x - first.astype(F32)
    second = rest.astype(BF16)
    return first, second, (rest - second.astype(F32)).astype(BF16)


def exact(a, b, a_dim, b_dim):
    a1, a2, a3 = thirds(a)
    b1, b2, b3 = thirds(b)
    left = jnp.concatenate([a1, a1, a2, a1, a2, a3], axis=a_dim)
    right = jnp.concatenate([b1, b2, b1, b3, b2, b1], axis=b_dim)
    return lax.dot_general(left, right, (((a_dim,), (b_dim,)), ((), ())), preferred_element_type=F32)


def exact_nt(a, b):
    return exact(a, b, 1, 1)


def exact_nn(a, b):
    return exact(a, b, 1, 0)


def halves(x):
    high = x.astype(BF16)
    return high, (x - high.astype(F32)).astype(BF16)


def product(a, b, contract):
    return lax.dot_general(a, b, (contract, ((), ())), preferred_element_type=F32)


def split_product(a, b, contract=((1,), (0,))):
    left = jnp.concatenate([a[0], a[0], a[1]], axis=contract[0][0])
    right = jnp.concatenate([b[0], b[1], b[0]], axis=contract[1][0])
    return product(left, right, contract)


def split_nt(a, b):
    return split_product(a, b, ((1,), (1,)))


def lane(x, k):
    return jnp.broadcast_to(x[:, k : k + 1], (8, 128))


def sub(x, k):
    return jnp.broadcast_to(x[k : k + 1, :], (8, 128))


def factor_block(rows, aside):
    rows, aside = list(rows), list(aside)
    sublane = lax.broadcasted_iota(jnp.int32, (8, 128), 0)
    half = GROUPS // 2
    for first, last in ((0, half), (half, GROUPS)):
        for s in range(first, last):
            cols = {b: [lane(rows[b], 8 * s + k) for k in range(8)] for b in range(s, last)}
            corner = [[sub(cols[s][k], i) if i >= k else None for k in range(8)] for i in range(8)]
            scale = None
            for k in range(8):
                r = 1.0 / corner[k][k]
                m = [corner[i][k] * r if i > k else None for i in range(8)]
                for i in range(k + 1, 8):
                    for j in range(k + 1, i + 1):
                        corner[i][j] = corner[i][j] - m[i] * corner[j][k]
                pivot_row = sub(rows[s], k)
                pivot_aside = sub(aside[s], k)
                for b in range(s, last):
                    mul = cols[b][k] * r
                    if b == s:
                        mul = jnp.where(sublane > k, mul, 0.0)
                    for j in range(k + 1, 8):
                        cols[b][j] = cols[b][j] - mul * corner[j][k]
                    rows[b] = rows[b] - mul * pivot_row
                    aside[b] = aside[b] - mul * pivot_aside
                y = lax.rsqrt(corner[k][k])
                y = y * (1.5 - 0.5 * corner[k][k] * y * y)
                scale = y if scale is None else jnp.where(sublane == k, y, scale)
            rows[s] = rows[s] * scale
            aside[s] = aside[s] * scale
        if first == 0:
            top = jnp.concatenate(rows[:half], axis=0)
            both = jnp.concatenate([top, jnp.concatenate(aside[:half], axis=0)], axis=1)
            change = exact(top, both, 0, 0)
            for b in range(half, GROUPS):
                rows[b] = rows[b] - change[8 * b : 8 * b + 8, :BLOCK]
                aside[b] = aside[b] - change[8 * b : 8 * b + 8, BLOCK:]
    return rows, aside


def merge(l_ref, x_ref, lo, h):
    a, b, c = lo, lo + h, lo + 2 * h
    t = exact_nn(l_ref[b:c, a:b], x_ref[a:b, a:b])
    x_ref[b:c, a:b] = -exact_nn(x_ref[b:c, b:c], t)


def forward(w_ref, l_ref, x_ref, lo, h):
    a, b, c = lo, lo + h, lo + 2 * h
    l21 = exact_nt(w_ref[b:c, a:b], x_ref[a:b, a:b])
    l_ref[b:c, a:b] = l21
    w_ref[b:c, b:c] = w_ref[b:c, b:c] - exact_nt(l21, l21)


def factor_blocks(w_ref, l_ref, x_ref):
    ri = lax.broadcasted_iota(jnp.int32, (BLOCK, BLOCK), 0)
    ci = lax.broadcasted_iota(jnp.int32, (BLOCK, BLOCK), 1)
    eye = jnp.where(ri == ci, 1.0, 0.0).astype(F32)

    def step(j, carry):
        block = pl.ds(pl.multiple_of(j * BLOCK, BLOCK), BLOCK)
        d = w_ref[block, block]
        cut = lambda v: [v[8 * b : 8 * b + 8] for b in range(GROUPS)]
        upper, inverse = factor_block(cut(d), cut(eye))
        l_ref[block, block] = jnp.where(ri >= ci, jnp.concatenate(upper, axis=0).T, 0.0)
        x_ref[block, block] = jnp.where(ri >= ci, jnp.concatenate(inverse, axis=0), 0.0)

        @pl.when(j == 0)
        def _():
            forward(w_ref, l_ref, x_ref, 0, BLOCK)

        return carry

    lax.fori_loop(0, HALF // BLOCK, step, 0)
    merge(l_ref, x_ref, 0, BLOCK)


def col_lanes(at_ref):
    col = at_ref[1]
    return [pl.ds(pl.multiple_of(lax.rem(col + N_Y - s, N_Y) * 128, 128), 128) for s in range(N_Y)]


def spread(at_ref, pieces, at_tile, out_ref):
    x, core = at_ref[2], at_ref[3]
    lanes = col_lanes(at_ref)
    for s_core in range(N_CORE):
        for s_x in range(N_X):
            piece = pieces[s_core * N_X + s_x]
            first = lax.rem(x + N_X - s_x, N_X) * N_Z * N_CORE + lax.rem(core + s_core, N_CORE)
            for z in range(N_Z):
                rows = pl.ds(pl.multiple_of((first + z * N_CORE) * 8, 8), 8)
                for s_y in range(N_Y):
                    out_ref[rows, lanes[s_y]] = piece[(z, s_y) + at_tile]


def first_half(*refs):
    at_ref, pieces = refs[0], refs[1:9]
    w_out, l_ref, x_ref, w_ref = refs[9:]
    spread(at_ref, pieces, (), w_ref)
    l_ref[...] = jnp.zeros((PIVOT, HALF), F32)
    x_ref[...] = jnp.zeros((HALF, HALF), F32)
    factor_blocks(w_ref, l_ref, x_ref)
    a = slice(0, HALF)
    b = slice(HALF, PIVOT)
    l21 = exact_nt(w_ref[b, a], x_ref[...])
    l_ref[b, :] = l21
    w_out[...] = w_ref[b, b] - exact_nt(l21, l21)


def second_half(w_in, l_in, x_in, l_ref, x_ref, w_ref, l22, x22):
    a = slice(0, HALF)
    b = slice(HALF, PIVOT)
    w_ref[...] = w_in[...]
    l22[...] = jnp.zeros((HALF, HALF), F32)
    x22[...] = jnp.zeros((HALF, HALF), F32)
    factor_blocks(w_ref, l22, x22)
    l_ref[:, a] = l_in[...]
    l_ref[a, b] = jnp.zeros((HALF, HALF), F32)
    l_ref[b, b] = l22[...]
    x_ref[a, a] = x_in[...]
    x_ref[a, b] = jnp.zeros((HALF, HALF), F32)
    x_ref[b, b] = x22[...]
    x_ref[b, a] = -exact_nn(x22[...], exact_nn(l_in[b, :], x_in[...]))


def times_upper(a, b):
    left = split_product([v[:, :HALF] for v in a], [v[:HALF, :HALF] for v in b])
    right = split_product(a, [v[:, HALF:] for v in b])
    return jnp.concatenate([left, right], axis=1)


def lower_times(a, b, contract):
    cut = (lambda v: v[:HALF]) if contract[1] == (0,) else (lambda v: v[:, :HALF])
    top = split_product([v[:HALF, :HALF] for v in a], [cut(v) for v in b], contract)
    bottom = split_product([v[HALF:] for v in a], b, contract)
    return jnp.concatenate([top, bottom], axis=0)


def tangent_factor(x_ref, ad_ref, phi_ref):
    h = HALF
    x11, x21, x22 = x_ref[:h, :h], x_ref[h:, :h], x_ref[h:, h:]
    t11 = exact_nn(x11, ad_ref[:h, :h])
    t21 = exact_nn(x21, ad_ref[:h, :h]) + exact_nn(x22, ad_ref[h:, :h])
    t22 = exact_nn(x21, ad_ref[:h, h:]) + exact_nn(x22, ad_ref[h:, h:])
    ri = lax.broadcasted_iota(jnp.int32, (h, h), 0)
    ci = lax.broadcasted_iota(jnp.int32, (h, h), 1)
    weight = jnp.where(ri > ci, 1.0, jnp.where(ri == ci, 0.5, 0.0)).astype(F32)
    phi_ref[:h, :h] = exact_nt(t11, x11) * weight
    phi_ref[h:, :h] = exact_nt(t21, x11)
    phi_ref[h:, h:] = (exact_nt(t21, x21) + exact_nt(t22, x22)) * weight
    phi_ref[:h, h:] = jnp.zeros((h, h), F32)


def panel(*refs):
    at_ref, l_ref, x_ref = refs[:3]
    pieces = refs[3:11]
    parts, tangent_parts = refs[11:15], refs[15:19]
    strip_ref, strip_tangent_ref = refs[19:21]
    factor_out, change_out, panel_out, panel_change_out, strip_out, strip_change_out = refs[21:27]
    ad, raw, phi, xs, phis, qs, qds, rows_ref, done_ref = refs[27:]
    col = at_ref[1]
    whole = slice(None)

    @pl.when(pl.program_id(0) == 0)
    def _():
        spread(at_ref, pieces, (0,), ad)
        spread(at_ref, pieces, (1,), raw.at[0])
        spread(at_ref, pieces, (2,), raw.at[1])
        tangent_factor(x_ref, ad, phi)
        own = pl.ds(pl.multiple_of(at_ref[0] * 8, 8), 8)
        lanes = pl.ds(pl.multiple_of(col * 128, 128), 128)
        factor_out[...] = l_ref[own, lanes]
        change_out[...] = exact_nn(l_ref[own, :], phi[:, lanes])
        inverse = halves(x_ref[...])
        xs[0], xs[1] = halves(x_ref[...].T)
        phis[0], phis[1] = halves(phi[...].T)
        solved = lower_times(inverse, halves(raw[...].reshape(2 * PIVOT, PIVOT)), ((1,), (1,)))
        q = halves(solved[:, :PIVOT])
        qs[0], qs[1] = q
        qds[0], qds[1] = halves(
            solved[:, PIVOT:] - lower_times(halves(phi[...]), q, ((1,), (0,)))
        )

    for shift, part, tangent_part in zip((0, 3, 1, 2), parts, tangent_parts):
        lanes = pl.ds(pl.multiple_of(lax.rem(col + shift, N_Y) * 128, 128), 128)
        for at, value in ((0, part[...]), (PANEL_TILE, tangent_part[...])):
            high, low = halves(value)
            rows_ref[0, at : at + PANEL_TILE, lanes] = high
            rows_ref[1, at : at + PANEL_TILE, lanes] = low
    solved = times_upper([rows_ref[0], rows_ref[1]], [xs[0], xs[1]])
    factor = solved[:PANEL_TILE]
    factor_halves = halves(factor)
    change = solved[PANEL_TILE:] - times_upper(factor_halves, [phis[0], phis[1]])
    change_halves = halves(change)
    done_ref[0] = factor
    done_ref[1] = change
    lanes = pl.ds(pl.multiple_of(col * 128, 128), 128)
    panel_out[...] = done_ref[0, :, lanes]
    panel_change_out[...] = done_ref[1, :, lanes]
    q = [qs[0], qs[1]]
    strip_out[...] = strip_ref[...] - split_product(factor_halves, q)
    strip_change_out[...] = strip_tangent_ref[...] - (
        split_product(change_halves, q) + split_product(factor_halves, [qds[0], qds[1]])
    )


def row_index(x, z, core):
    return (x % N_X * N_Z + z % N_Z) * N_CORE + core % N_CORE


ALONG_Z = [
    [row_index(x, z, core) for z in range(N_Z)] for x in range(N_X) for core in range(N_CORE)
]

def along_y(value, s):
    return lax.ppermute(value, "col", [(c, (c + s) % N_Y) for c in range(N_Y)])


def along_x_core(value, s_x, s_core):
    pairs = [
        (row_index(x, z, core), row_index(x + s_x, z, core + s_core))
        for x in range(N_X)
        for z in range(N_Z)
        for core in range(N_CORE)
    ]
    return lax.ppermute(value, "row", pairs)


def gather_z(value):
    spread = jnp.broadcast_to(value[None], (N_Z,) + value.shape)
    return lax.all_to_all(spread, "row", 0, 0, axis_index_groups=ALONG_Z)


def vmem_spec():
    return pl.BlockSpec(memory_space=pltpu.VMEM)


def smem_spec():
    return pl.BlockSpec(memory_space=pltpu.SMEM)


def matrix(*shape):
    return jax.ShapeDtypeStruct(shape, F32)


LIMIT = pltpu.CompilerParams(vmem_limit_bytes=56 * 2**20)


def run_panel(at, whole_factor, inverse, rest_pieces, parts, tangent_parts, strip_block, strip_tangent):
    local_rows, local_strip = strip_block.shape
    tile = PANEL_TILE
    narrow = pl.BlockSpec((tile, 128), lambda i: (i, 0))
    broad = pl.BlockSpec((tile, local_strip), lambda i: (i, 0))
    corner = pl.BlockSpec((8, 128), lambda i: (0, 0))
    square = pltpu.VMEM((PIVOT, PIVOT), F32)
    split_square = pltpu.VMEM((2, PIVOT, PIVOT), BF16)
    return pl.pallas_call(
        panel,
        name="panel",
        grid=(local_rows // tile,),
        out_shape=(
            matrix(8, 128),
            matrix(8, 128),
            matrix(local_rows, 128),
            matrix(local_rows, 128),
            matrix(local_rows, local_strip),
            matrix(local_rows, local_strip),
        ),
        in_specs=[smem_spec()] + [vmem_spec()] * 10 + [narrow] * 8 + [broad] * 2,
        out_specs=(corner, corner, narrow, narrow, broad, broad),
        scratch_shapes=[
            square,
            pltpu.VMEM((2, PIVOT, PIVOT), F32),
            square,
            split_square,
            split_square,
            split_square,
            split_square,
            pltpu.VMEM((2, 2 * tile, PIVOT), BF16),
            pltpu.VMEM((2, tile, PIVOT), F32),
        ],
        compiler_params=LIMIT,
        cost_estimate=pl.CostEstimate(flops=10**10, bytes_accessed=20 * 10**6, transcendentals=0),
    )(at, whole_factor, inverse, *rest_pieces, *parts, *tangent_parts, strip_block, strip_tangent)


def body(pivot_block, pivot_tangent, panel_block, panel_tangent, strip_block, strip_tangent):
    row = lax.axis_index("row")
    col = lax.axis_index("col")
    at = jnp.stack([row, col, row // (N_Z * N_CORE), row % N_CORE]).astype(jnp.int32)

    def tiles(s):
        at_row = lax.rem(col + s, N_Y) * 8
        return jnp.stack(
            [
                pivot_block,
                pivot_tangent,
                lax.dynamic_slice_in_dim(panel_block, at_row, 8, 0),
                lax.dynamic_slice_in_dim(panel_tangent, at_row, 8, 0),
            ]
        )

    by_y = [tiles(0)] + [along_y(tiles(s), s) for s in range(1, N_Y)]
    gathered = gather_z(jnp.stack(by_y))
    pivot, rest = gathered[:, :, 0], gathered[:, :, 1:]
    pivot_pieces = [pivot] + [along_x_core(pivot, s, 0) for s in range(1, N_X)]
    pivot_pieces = pivot_pieces + [along_x_core(v, 0, 1) for v in pivot_pieces]
    own_core = [rest] + [along_x_core(rest, s, 0) for s in range(1, N_X)]
    rest_pieces = own_core + [along_x_core(v, 0, 1) for v in own_core]

    def around(value, forward_first):
        left, right = along_y(value, 1), along_y(value, 3)
        far = along_y(left, 1) if forward_first else along_y(right, 3)
        return [value, left, right, far]

    parts = around(panel_block, True)
    tangent_parts = around(panel_tangent, False)

    w22, l_left, x_first = pl.pallas_call(
        first_half,
        name="first_half",
        out_shape=(matrix(HALF, HALF), matrix(PIVOT, HALF), matrix(HALF, HALF)),
        in_specs=[smem_spec()] + [vmem_spec()] * 8,
        out_specs=[vmem_spec()] * 3,
        scratch_shapes=[pltpu.VMEM((PIVOT, PIVOT), F32)],
        compiler_params=LIMIT,
        cost_estimate=pl.CostEstimate(flops=16 * 10**9, bytes_accessed=10**6, transcendentals=0),
    )(at, *pivot_pieces)
    whole_factor, inverse = pl.pallas_call(
        second_half,
        name="second_half",
        out_shape=(matrix(PIVOT, PIVOT), matrix(PIVOT, PIVOT)),
        in_specs=[vmem_spec()] * 3,
        out_specs=[vmem_spec()] * 2,
        scratch_shapes=[pltpu.VMEM((HALF, HALF), F32)] * 3,
        compiler_params=LIMIT,
        cost_estimate=pl.CostEstimate(flops=16 * 10**9, bytes_accessed=10**6, transcendentals=0),
    )(w22, l_left, x_first)

    return run_panel(
        at, whole_factor, inverse, rest_pieces, parts, tangent_parts, strip_block, strip_tangent
    )


def solution(mesh):
    spec = P("row", "col")
    return jax.shard_map(
        body, mesh=mesh, in_specs=(spec,) * 6, out_specs=(spec,) * 6, check_vma=False
    )
```

time: 113 us -> 109 us (0.965)
  Pallas kernels: 52.4 us -> 45.8 us
  waiting for transfers between devices: 14.8 us -> 16.8 us
    pallas_call x1, Pallas kernels: 23.9 us -> 21.3 us  [run_panel(): pl.pallas_call(panel, name='panel', grid=(local_rows // tile,), out_shape...]
    pallas_call x1, Pallas kernels: 14.3 us -> 12.2 us  [body(): pl.pallas_call(second_half, name='second_half', out_shape=(matrix(PIVOT,...]
    pallas_call x1, Pallas kernels: 14.2 us -> 12.2 us  [body(): pl.pallas_call(first_half, name='first_half', out_shape=(matrix(HALF, HAL...]
    ppermute x14, waiting for transfers between devices: 0.56 us -> 2.54 us  [along_x_core(): return lax.ppermute(value, 'row', pairs)]
  transfers between devices with their start and end apart: 24 -> 24, of which waited for: 4 -> 4; matrix products, arithmetic and copies ran while one was open for 1% -> 1% of each run, Pallas kernels for 25% -> 23%
where the time goes in v1:
time: 109 us
  Pallas kernels  45.8 us (42%)
  starting transfers between devices  39.7 us (36%)
  waiting for transfers between devices  16.8 us (15%)
  local copies, waits for them, and re-layouts  3.82 us (4%)
  other arithmetic  1.29 us (1%)
  between operations  1.11 us (1%)
    pallas_call x1, Pallas kernels, run_panel(): pl.pallas_call(panel, name='panel', grid=(local_rows // tile,), out_shape...  21.3 us
    ppermute x14, starting transfers between devices, along_x_core(): return lax.ppermute(value, 'row', pairs)  18.3 us
    ppermute x9, starting transfers between devices, along_y(): return lax.ppermute(value, 'col', [(c, (c + s) % N_Y) for c in range(N_Y)])  13.2 us
    all_to_all x1, waiting for transfers between devices, gather_z(): return lax.all_to_all(spread, 'row', 0, 0, axis_index_groups=ALONG_Z)  12.4 us
    pallas_call x1, Pallas kernels, body(): pl.pallas_call(first_half, name='first_half', out_shape=(matrix(HALF, HAL...  12.2 us
    pallas_call x1, Pallas kernels, body(): pl.pallas_call(second_half, name='second_half', out_shape=(matrix(PIVOT,...  12.2 us
    all_to_all x1, starting transfers between devices, gather_z(): return lax.all_to_all(spread, 'row', 0, 0, axis_index_groups=ALONG_Z)  8.19 us
    ppermute x14, waiting for transfers between devices, along_x_core(): return lax.ppermute(value, 'row', pairs)  2.54 us
  transfers between devices with their start and end apart: 24, of which 4 were waited for; matrix products, arithmetic and copies ran while one was open for 1% of the time, Pallas kernels for 23%

profile of v1, /device:TPU:1, one launch (start us, length us, event | category | flops | bytes accessed | tf_op | source)
XLA Modules:
  0.0 108.5 jit_solution(10278645901601846102)
XLA Ops:
  0.6 0.0 copy-start.2
  0.7 0.8 dynamic-slice_bitcast_fusion.7
  1.5 0.7 dynamic-slice_bitcast_fusion.6
  2.2 0.7 maximum_bitcast_fusion
  2.9 2.1 %collective-permute-start = (f32[4,8,128]{2,1,0:T(8,128)S(1)}, f32[4,8,128]{2,1,0:T(8,128)S(1)}, u32[]{:S(2)}, u32[]{:S(2)}) collective-permute-start(f32[4,8,128]{2,1,0:T(8,128)S(1)} %get-tuple-element.25), channel_id=1, source_target_pairs={{0,1},{1,2},{2,3},{3,0},{4,5},{5,6},{6,7},{7,4},{8,9},{9,10},{10,1... | collective-permute-start | bytes 49160 | tf_op jit(solution)/shard_map/ppermute | solution.py:282
  5.0 2.6 %collective-permute-start.1 = (f32[4,8,128]{2,1,0:T(8,128)S(1)}, f32[4,8,128]{2,1,0:T(8,128)S(1)}, u32[]{:S(2)}, u32[]{:S(2)}) collective-permute-start(f32[4,8,128]{2,1,0:T(8,128)S(1)} %get-tuple-element.26), channel_id=1, source_target_pairs={{0,2},{1,3},{2,0},{3,1},{4,6},{5,7},{6,4},{7,5},{8,10},{9,11},{10,... | collective-permute-start | bytes 49160 | tf_op jit(solution)/shard_map/ppermute | solution.py:282
  7.7 1.1 collective-permute-start.2
  8.7 0.4 collective-permute-done.1
  9.1 1.4 %collective-permute-done.2 = f32[4,8,128]{2,1,0:T(8,128)S(1)} collective-permute-done((f32[4,8,128]{2,1,0:T(8,128)S(1)}, f32[4,8,128]{2,1,0:T(8,128)S(1)}, u32[]{:S(2)}, u32[]{:S(2)}) %collective-permute-start.2) | collective-permute-done | bytes 16416 | tf_op jit(solution)/shard_map/ppermute | solution.py:282
  10.6 0.9 broadcast_in_dim.2
  11.4 8.2 %all-to-all-start = ((f32[8,4,4,8,128]{4,3,2,1,0:T(8,128)}), f32[8,4,4,8,128]{4,3,2,1,0:T(8,128)S(1)}, u32[]{:S(2)}, u32[]{:S(2)}) async-start(f32[8,4,4,8,128]{4,3,2,1,0:T(8,128)} %broadcast_in_dim.2), calls=%async_computation | async-start | bytes 1048576 | tf_op jit(solution)/shard_map/all_to_all | solution.py:297
  19.6 0.0 collective-permute-start.17
  19.6 2.7 %collective-permute-start.18 = (f32[1024,128]{1,0:T(8,128)}, f32[1024,128]{1,0:T(8,128)S(1)}, u32[]{:S(2)}, u32[]{:S(2)}) collective-permute-start(f32[1024,128]{1,0:T(8,128)} %refs_11_.1), channel_id=1, source_target_pairs={{0,3},{1,0},{2,1},{3,2},{4,7},{5,4},{6,5},{7,6},{8,11},{9,8},{10,9... | collective-permute-start | bytes 1572872 | tf_op jit(solution)/shard_map/ppermute | solution.py:282
  22.3 12.4 %all-to-all-done = f32[8,4,4,8,128]{4,3,2,1,0:T(8,128)S(1)} async-done(((f32[8,4,4,8,128]{4,3,2,1,0:T(8,128)}), f32[8,4,4,8,128]{4,3,2,1,0:T(8,128)S(1)}, u32[]{:S(2)}, u32[]{:S(2)}) %all-to-all-start) | async-done | bytes 524320 | tf_op jit(solution)/shard_map/all_to_all | solution.py:297
  34.7 0.0 copy-start.1
  34.8 2.6 %collective-permute-start.5 = (f32[8,4,8,128]{3,2,1,0:T(8,128)S(1)}, f32[8,4,8,128]{3,2,1,0:T(8,128)S(1)}, u32[]{:S(2)}, u32[]{:S(2)}) collective-permute-start(f32[8,4,8,128]{3,2,1,0:T(8,128)S(1)} %slice_bitcast_fusion.refs_1_), channel_id=1, source_target_pairs={{0,192},{4,196},{8,200},{12,204},{16,208},{20,212},{24,216},{28,22... | collective-permute-start | bytes 393224 | tf_op jit(solution)/shard_map/ppermute | solution.py:292
  37.3 0.5 collective-permute-start.4
  37.8 0.6 collective-permute-start.3
  38.4 0.0 collective-permute-done.18.refs_13_
  38.4 4.2 %collective-permute-start.6 = (f32[8,4,8,128]{3,2,1,0:T(8,128)S(1)}, f32[8,4,8,128]{3,2,1,0:T(8,128)S(1)}, u32[]{:S(2)}, u32[]{:S(2)}) collective-permute-start(f32[8,4,8,128]{3,2,1,0:T(8,128)S(1)} %slice_bitcast_fusion.refs_1_), channel_id=1, source_target_pairs={{0,4},{4,0},{8,12},{12,8},{16,20},{20,16},{24,28},{28,24},{32,36},... | collective-permute-start | bytes 393224 | tf_op jit(solution)/shard_map/ppermute | solution.py:292
  42.6 0.0 collective-permute-done.5.refs_4_
  42.6 2.2 %collective-permute-start.9 = (f32[8,4,8,128]{3,2,1,0:T(8,128)S(1)}, f32[8,4,8,128]{3,2,1,0:T(8,128)S(1)}, u32[]{:S(2)}, u32[]{:S(2)}) collective-permute-start(f32[8,4,8,128]{3,2,1,0:T(8,128)S(1)} %collective-permute-done.5.refs_4_), channel_id=1, source_target_pairs={{0,4},{4,0},{8,12},{12,8},{16,20},{20,16},{24,28},{28,24},{32,36},... | collective-permute-start | bytes 393224 | tf_op jit(solution)/shard_map/ppermute | solution.py:292
  44.8 0.0 collective-permute-done.4.refs_3_
  44.8 2.6 %collective-permute-start.8 = (f32[8,4,8,128]{3,2,1,0:T(8,128)S(1)}, f32[8,4,8,128]{3,2,1,0:T(8,128)S(1)}, u32[]{:S(2)}, u32[]{:S(2)}) collective-permute-start(f32[8,4,8,128]{3,2,1,0:T(8,128)S(1)} %collective-permute-done.4.refs_3_), channel_id=1, source_target_pairs={{0,4},{4,0},{8,12},{12,8},{16,20},{20,16},{24,28},{28,24},{32,36},... | collective-permute-start | bytes 393224 | tf_op jit(solution)/shard_map/ppermute | solution.py:292
  47.5 1.3 %collective-permute-start.7 = (f32[8,4,8,128]{3,2,1,0:T(8,128)S(1)}, f32[8,4,8,128]{3,2,1,0:T(8,128)}, u32[]{:S(2)}, u32[]{:S(2)}) collective-permute-start(f32[8,4,8,128]{3,2,1,0:T(8,128)S(1)} %collective-permute-done.3.refs_2_), channel_id=1, source_target_pairs={{0,4},{4,0},{8,12},{12,8},{16,20},{20,16},{24,28},{28,24},{32,36},... | collective-permute-start | bytes 393224 | tf_op jit(solution)/shard_map/ppermute | solution.py:292
  48.8 0.6 pad_add_fusion.refs_0_
  49.5 2.1 %collective-permute-start.21 = (f32[1024,128]{1,0:T(8,128)S(1)}, f32[1024,128]{1,0:T(8,128)S(1)}, u32[]{:S(2)}, u32[]{:S(2)}) collective-permute-start(f32[1024,128]{1,0:T(8,128)S(1)} %copy-done.2), channel_id=1, source_target_pairs={{0,3},{1,0},{2,1},{3,2},{4,7},{5,4},{6,5},{7,6},{8,11},{9,8},{10,9... | collective-permute-start | bytes 1572872 | tf_op jit(solution)/shard_map/ppermute | solution.py:282
  51.5 0.0 collective-permute-done.6.refs_5_
  51.5 0.0 collective-permute-start.19
  51.5 0.4 collective-permute-start.12
  51.9 0.5 collective-permute-start.11
  52.4 0.9 collective-permute-start.10
  53.4 12.2 %first_half.1 = (f32[256,256]{1,0:T(8,128)}, f32[512,256]{1,0:T(8,128)}, f32[256,256]{1,0:T(8,128)}) custom-call(s32[4]{0:T(128)} %pad_add_fusion.refs_0_, f32[8,4,8,128]{3,2,1,0:T(8,128)} %copy-done.1, f32[8,4,8,128]{3,2,1,0:T(8,128)} %copy-done.18, f32[8,4,8,128]{3,2,1,0:T(8,128)} %copy-done.17, f32[8,4,8,128]{3,2,1,0:T(8,128)} %copy-done.16, ...), custom_call_target="tpu_custom_call" | custom-call | flops 16000000000 | bytes 1000000 | tf_op jit(solution)/shard_map/first_half/pallas_call | solution.py:385
  65.7 2.7 %collective-permute-start.22 = (f32[1024,128]{1,0:T(8,128)S(1)}, f32[1024,128]{1,0:T(8,128)S(1)}, u32[]{:S(2)}, u32[]{:S(2)}) collective-permute-start(f32[1024,128]{1,0:T(8,128)S(1)} %collective-permute-done.21.refs_17_), channel_id=1, source_target_pairs={{0,3},{1,0},{2,1},{3,2},{4,7},{5,4},{6,5},{7,6},{8,11},{9,8},{10,9... | collective-permute-start | bytes 1572872 | tf_op jit(solution)/shard_map/ppermute | solution.py:282
  68.4 1.5 %collective-permute-start.13 = (f32[8,4,3,8,128]{4,3,2,1,0:T(8,128)S(1)}, f32[8,4,3,8,128]{4,3,2,1,0:T(8,128)S(1)}, u32[]{:S(2)}, u32[]{:S(2)}) collective-permute-start(f32[8,4,3,8,128]{4,3,2,1,0:T(8,128)S(1)} %slice.9.refs_3_), channel_id=1, source_target_pairs={{0,4},{4,0},{8,12},{12,8},{16,20},{20,16},{24,28},{28,24},{32,36},... | collective-permute-start | bytes 1179656 | tf_op jit(solution)/shard_map/ppermute | solution.py:292
  69.9 0.0 collective-permute-done.12.refs_6_
  69.9 0.1 collective-permute-start.16
  70.0 0.0 collective-permute-done.11.refs_5_
  70.0 0.4 collective-permute-start.15
  70.4 2.5 %collective-permute-done.10.refs_4_ = f32[8,4,3,8,128]{4,3,2,1,0:T(8,128)S(1)} collective-permute-done((f32[8,4,3,8,128]{4,3,2,1,0:T(8,128)S(1)}, f32[8,4,3,8,128]{4,3,2,1,0:T(8,128)S(1)}, u32[]{:S(2)}, u32[]{:S(2)}) %collective-permute-start.10) | collective-permute-done | bytes 393248 | tf_op jit(solution)/shard_map/ppermute | solution.py:292
  72.9 0.5 collective-permute-start.14
  73.4 12.2 %second_half.1 = (f32[512,512]{1,0:T(8,128)}, f32[512,512]{1,0:T(8,128)}) custom-call(f32[256,256]{1,0:T(8,128)} %get-tuple-element.11.w_in, f32[512,256]{1,0:T(8,128)} %get-tuple-element.12.l_in, f32[256,256]{1,0:T(8,128)} %get-tuple-element.13.x_in), custom_call_target="tpu_custom_call" | custom-call | flops 16000000000 | bytes 1000000 | tf_op jit(solution)/shard_map/second_half/pallas_call | solution.py:395
  85.7 0.7 copy-done.8
  86.5 0.1 copy-done.12
  86.6 0.1 copy-done.13
  86.7 0.1 copy-done.14
  86.8 0.2 copy-done.15
  87.0 21.3 %panel.1 = (f32[8,128]{1,0:T(8,128)}, f32[8,128]{1,0:T(8,128)}, f32[1024,128]{1,0:T(8,128)}, f32[1024,128]{1,0:T(8,128)}, f32[1024,512]{1,0:T(8,128)}, /*index=5*/f32[1024,512]{1,0:T(8,128)}) custom-call(s32[4]{0:T(128)} %pad_add_fusion.refs_0_, f32[512,512]{1,0:T(8,128)} %get-tuple-element.14.refs_1_, f32[512,512]{1,0:T(8,128)} %get-tuple-element.15.refs_2_, ...), custom_call_target="tpu_custom_call" | custom-call | flops 10000000000 | bytes 20000000 | tf_op jit(solution)/shard_map/panel/pallas_call | solution.py:323
  (55 shorter events, 0.2 us)
Async XLA Ops:
  0.6 48.8 %copy-start.2 = (f32[1024,128]{1,0:T(8,128)S(1)}, f32[1024,128]{1,0:T(8,128)}, u32[]{:S(2)}) copy-start(f32[1024,128]{1,0:T(8,128)} %refs_15_.1) | copy-start | bytes 1572868
  2.9 5.8 %collective-permute-start = (f32[4,8,128]{2,1,0:T(8,128)S(1)}, f32[4,8,128]{2,1,0:T(8,128)S(1)}, u32[]{:S(2)}, u32[]{:S(2)}) collective-permute-start(f32[4,8,128]{2,1,0:T(8,128)S(1)} %get-tuple-element.25), channel_id=1, source_target_pairs={{0,1},{1,2},{2,3},{3,0},{4,5},{5,6},{6,7},{7,4},{8,9},{9,10},{10,1... | collective-permute-start | bytes 49160 | tf_op jit(solution)/shard_map/ppermute | solution.py:282
  5.0 4.1 %collective-permute-start.1 = (f32[4,8,128]{2,1,0:T(8,128)S(1)}, f32[4,8,128]{2,1,0:T(8,128)S(1)}, u32[]{:S(2)}, u32[]{:S(2)}) collective-permute-start(f32[4,8,128]{2,1,0:T(8,128)S(1)} %get-tuple-element.26), channel_id=1, source_target_pairs={{0,2},{1,3},{2,0},{3,1},{4,6},{5,7},{6,4},{7,5},{8,10},{9,11},{10,... | collective-permute-start | bytes 49160 | tf_op jit(solution)/shard_map/ppermute | solution.py:282
  7.7 2.9 %collective-permute-start.2 = (f32[4,8,128]{2,1,0:T(8,128)S(1)}, f32[4,8,128]{2,1,0:T(8,128)S(1)}, u32[]{:S(2)}, u32[]{:S(2)}) collective-permute-start(f32[4,8,128]{2,1,0:T(8,128)S(1)} %get-tuple-element.27), channel_id=1, source_target_pairs={{0,3},{1,0},{2,1},{3,2},{4,7},{5,4},{6,5},{7,6},{8,11},{9,8},{10,9... | collective-permute-start | bytes 49160 | tf_op jit(solution)/shard_map/ppermute | solution.py:282
  11.4 23.3 %all-to-all-start = ((f32[8,4,4,8,128]{4,3,2,1,0:T(8,128)}), f32[8,4,4,8,128]{4,3,2,1,0:T(8,128)S(1)}, u32[]{:S(2)}, u32[]{:S(2)}) async-start(f32[8,4,4,8,128]{4,3,2,1,0:T(8,128)} %broadcast_in_dim.2), calls=%async_computation | async-start | bytes 1048576 | tf_op jit(solution)/shard_map/all_to_all | solution.py:297
  19.6 18.2 %collective-permute-start.17 = (f32[1024,128]{1,0:T(8,128)}, f32[1024,128]{1,0:T(8,128)S(1)}, u32[]{:S(2)}, u32[]{:S(2)}) collective-permute-start(f32[1024,128]{1,0:T(8,128)} %refs_11_.1), channel_id=1, source_target_pairs={{0,1},{1,2},{2,3},{3,0},{4,5},{5,6},{6,7},{7,4},{8,9},{9,10},{10,1... | collective-permute-start | bytes 1572872 | tf_op jit(solution)/shard_map/ppermute | solution.py:282
  19.6 18.8 %collective-permute-start.18 = (f32[1024,128]{1,0:T(8,128)}, f32[1024,128]{1,0:T(8,128)S(1)}, u32[]{:S(2)}, u32[]{:S(2)}) collective-permute-start(f32[1024,128]{1,0:T(8,128)} %refs_11_.1), channel_id=1, source_target_pairs={{0,3},{1,0},{2,1},{3,2},{4,7},{5,4},{6,5},{7,6},{8,11},{9,8},{10,9... | collective-permute-start | bytes 1572872 | tf_op jit(solution)/shard_map/ppermute | solution.py:282
  22.3 27.2 %collective-permute-start.20 = (f32[1024,128]{1,0:T(8,128)}, f32[1024,128]{1,0:T(8,128)S(1)}, u32[]{:S(2)}, u32[]{:S(2)}) collective-permute-start(f32[1024,128]{1,0:T(8,128)} %refs_15_.1), channel_id=1, source_target_pairs={{0,1},{1,2},{2,3},{3,0},{4,5},{5,6},{6,7},{7,4},{8,9},{9,10},{10,1... | collective-permute-start | bytes 1572872 | tf_op jit(solution)/shard_map/ppermute | solution.py:282
  34.7 18.6 %copy-start.1 = (f32[8,4,8,128]{3,2,1,0:T(8,128)}, f32[8,4,8,128]{3,2,1,0:T(8,128)S(1)}, u32[]{:S(2)}) copy-start(f32[8,4,8,128]{3,2,1,0:T(8,128)S(1)} %slice_bitcast_fusion.refs_1_) | copy-start | bytes 393220
  34.8 7.9 %collective-permute-start.5 = (f32[8,4,8,128]{3,2,1,0:T(8,128)S(1)}, f32[8,4,8,128]{3,2,1,0:T(8,128)S(1)}, u32[]{:S(2)}, u32[]{:S(2)}) collective-permute-start(f32[8,4,8,128]{3,2,1,0:T(8,128)S(1)} %slice_bitcast_fusion.refs_1_), channel_id=1, source_target_pairs={{0,192},{4,196},{8,200},{12,204},{16,208},{20,212},{24,216},{28,22... | collective-permute-start | bytes 393224 | tf_op jit(solution)/shard_map/ppermute | solution.py:292
  37.3 7.5 %collective-permute-start.4 = (f32[8,4,8,128]{3,2,1,0:T(8,128)S(1)}, f32[8,4,8,128]{3,2,1,0:T(8,128)S(1)}, u32[]{:S(2)}, u32[]{:S(2)}) collective-permute-start(f32[8,4,8,128]{3,2,1,0:T(8,128)S(1)} %slice_bitcast_fusion.refs_1_), channel_id=1, source_target_pairs={{0,128},{4,132},{8,136},{12,140},{16,144},{20,148},{24,152},{28,15... | collective-permute-start | bytes 393224 | tf_op jit(solution)/shard_map/ppermute | solution.py:292
  37.8 27.8 %copy-start.3 = (f32[1024,128]{1,0:T(8,128)}, f32[1024,128]{1,0:T(8,128)S(1)}, u32[]{:S(2)}) copy-start(f32[1024,128]{1,0:T(8,128)S(1)} %collective-permute-done.17.refs_12_) | copy-start | bytes 1572868
  37.8 9.7 %collective-permute-start.3 = (f32[8,4,8,128]{3,2,1,0:T(8,128)S(1)}, f32[8,4,8,128]{3,2,1,0:T(8,128)S(1)}, u32[]{:S(2)}, u32[]{:S(2)}) collective-permute-start(f32[8,4,8,128]{3,2,1,0:T(8,128)S(1)} %slice_bitcast_fusion.refs_1_), channel_id=1, source_target_pairs={{0,64},{4,68},{8,72},{12,76},{16,80},{20,84},{24,88},{28,92},{32,9... | collective-permute-start | bytes 393224 | tf_op jit(solution)/shard_map/ppermute | solution.py:292
  38.4 27.2 %copy-start.4 = (f32[1024,128]{1,0:T(8,128)}, f32[1024,128]{1,0:T(8,128)S(1)}, u32[]{:S(2)}) copy-start(f32[1024,128]{1,0:T(8,128)S(1)} %collective-permute-done.18.refs_13_) | copy-start | bytes 1572868
  38.4 13.1 %collective-permute-start.6 = (f32[8,4,8,128]{3,2,1,0:T(8,128)S(1)}, f32[8,4,8,128]{3,2,1,0:T(8,128)S(1)}, u32[]{:S(2)}, u32[]{:S(2)}) collective-permute-start(f32[8,4,8,128]{3,2,1,0:T(8,128)S(1)} %slice_bitcast_fusion.refs_1_), channel_id=1, source_target_pairs={{0,4},{4,0},{8,12},{12,8},{16,20},{20,16},{24,28},{28,24},{32,36},... | collective-permute-start | bytes 393224 | tf_op jit(solution)/shard_map/ppermute | solution.py:292
  42.6 10.8 %copy-start.16 = (f32[8,4,8,128]{3,2,1,0:T(8,128)}, f32[8,4,8,128]{3,2,1,0:T(8,128)S(1)}, u32[]{:S(2)}) copy-start(f32[8,4,8,128]{3,2,1,0:T(8,128)S(1)} %collective-permute-done.5.refs_4_) | copy-start | bytes 393220
  42.6 8.9 %collective-permute-start.9 = (f32[8,4,8,128]{3,2,1,0:T(8,128)S(1)}, f32[8,4,8,128]{3,2,1,0:T(8,128)S(1)}, u32[]{:S(2)}, u32[]{:S(2)}) collective-permute-start(f32[8,4,8,128]{3,2,1,0:T(8,128)S(1)} %collective-permute-done.5.refs_4_), channel_id=1, source_target_pairs={{0,4},{4,0},{8,12},{12,8},{16,20},{20,16},{24,28},{28,24},{32,36},... | collective-permute-start | bytes 393224 | tf_op jit(solution)/shard_map/ppermute | solution.py:292
  44.8 8.5 %copy-start.17 = (f32[8,4,8,128]{3,2,1,0:T(8,128)}, f32[8,4,8,128]{3,2,1,0:T(8,128)S(1)}, u32[]{:S(2)}) copy-start(f32[8,4,8,128]{3,2,1,0:T(8,128)S(1)} %collective-permute-done.4.refs_3_) | copy-start | bytes 393220
  44.8 7.1 %collective-permute-start.8 = (f32[8,4,8,128]{3,2,1,0:T(8,128)S(1)}, f32[8,4,8,128]{3,2,1,0:T(8,128)S(1)}, u32[]{:S(2)}, u32[]{:S(2)}) collective-permute-start(f32[8,4,8,128]{3,2,1,0:T(8,128)S(1)} %collective-permute-done.4.refs_3_), channel_id=1, source_target_pairs={{0,4},{4,0},{8,12},{12,8},{16,20},{20,16},{24,28},{28,24},{32,36},... | collective-permute-start | bytes 393224 | tf_op jit(solution)/shard_map/ppermute | solution.py:292
  47.5 5.9 %copy-start.18 = (f32[8,4,8,128]{3,2,1,0:T(8,128)}, f32[8,4,8,128]{3,2,1,0:T(8,128)S(1)}, u32[]{:S(2)}) copy-start(f32[8,4,8,128]{3,2,1,0:T(8,128)S(1)} %collective-permute-done.3.refs_2_) | copy-start | bytes 393220
  47.5 4.9 %collective-permute-start.7 = (f32[8,4,8,128]{3,2,1,0:T(8,128)S(1)}, f32[8,4,8,128]{3,2,1,0:T(8,128)}, u32[]{:S(2)}, u32[]{:S(2)}) collective-permute-start(f32[8,4,8,128]{3,2,1,0:T(8,128)S(1)} %collective-permute-done.3.refs_2_), channel_id=1, source_target_pairs={{0,4},{4,0},{8,12},{12,8},{16,20},{20,16},{24,28},{28,24},{32,36},... | collective-permute-start | bytes 393224 | tf_op jit(solution)/shard_map/ppermute | solution.py:292
  49.4 18.9 %copy-start = (f32[8,4,3,8,128]{4,3,2,1,0:T(8,128)}, f32[8,4,3,8,128]{4,3,2,1,0:T(8,128)S(1)}, u32[]{:S(2)}) copy-start(f32[8,4,3,8,128]{4,3,2,1,0:T(8,128)S(1)} %slice.9.refs_3_) | copy-start | bytes 1179652
  49.4 16.2 %copy-start.5 = (f32[1024,128]{1,0:T(8,128)}, f32[1024,128]{1,0:T(8,128)S(1)}, u32[]{:S(2)}) copy-start(f32[1024,128]{1,0:T(8,128)S(1)} %collective-permute-done.20.refs_16_) | copy-start | bytes 1572868
  49.5 16.2 %collective-permute-start.21 = (f32[1024,128]{1,0:T(8,128)S(1)}, f32[1024,128]{1,0:T(8,128)S(1)}, u32[]{:S(2)}, u32[]{:S(2)}) collective-permute-start(f32[1024,128]{1,0:T(8,128)S(1)} %copy-done.2), channel_id=1, source_target_pairs={{0,3},{1,0},{2,1},{3,2},{4,7},{5,4},{6,5},{7,6},{8,11},{9,8},{10,9... | collective-permute-start | bytes 1572872 | tf_op jit(solution)/shard_map/ppermute | solution.py:282
  51.5 1.9 %copy-start.19 = (f32[8,4,8,128]{3,2,1,0:T(8,128)}, f32[8,4,8,128]{3,2,1,0:T(8,128)S(1)}, u32[]{:S(2)}) copy-start(f32[8,4,8,128]{3,2,1,0:T(8,128)S(1)} %collective-permute-done.6.refs_5_) | copy-start | bytes 393220
  51.5 16.8 %collective-permute-start.19 = (f32[1024,128]{1,0:T(8,128)S(1)}, f32[1024,128]{1,0:T(8,128)S(1)}, u32[]{:S(2)}, u32[]{:S(2)}) collective-permute-start(f32[1024,128]{1,0:T(8,128)S(1)} %collective-permute-done.17.refs_12_), channel_id=1, source_target_pairs={{0,1},{1,2},{2,3},{3,0},{4,5},{5,6},{6,7},{7,4},{8,9},{9,10},{10,1... | collective-permute-start | bytes 1572872 | tf_op jit(solution)/shard_map/ppermute | solution.py:282
  51.5 1.9 %copy-start.20 = (f32[8,4,8,128]{3,2,1,0:T(8,128)}, f32[8,4,8,128]{3,2,1,0:T(8,128)S(1)}, u32[]{:S(2)}) copy-start(f32[8,4,8,128]{3,2,1,0:T(8,128)S(1)} %collective-permute-done.9.refs_8_) | copy-start | bytes 393220
  51.5 18.3 %collective-permute-start.12 = (f32[8,4,3,8,128]{4,3,2,1,0:T(8,128)S(1)}, f32[8,4,3,8,128]{4,3,2,1,0:T(8,128)S(1)}, u32[]{:S(2)}, u32[]{:S(2)}) collective-permute-start(f32[8,4,3,8,128]{4,3,2,1,0:T(8,128)S(1)} %slice.9.refs_3_), channel_id=1, source_target_pairs={{0,192},{4,196},{8,200},{12,204},{16,208},{20,212},{24,216},{28,22... | collective-permute-start | bytes 1179656 | tf_op jit(solution)/shard_map/ppermute | solution.py:292
  51.9 1.5 %copy-start.21 = (f32[8,4,8,128]{3,2,1,0:T(8,128)}, f32[8,4,8,128]{3,2,1,0:T(8,128)S(1)}, u32[]{:S(2)}) copy-start(f32[8,4,8,128]{3,2,1,0:T(8,128)S(1)} %collective-permute-done.8.refs_7_) | copy-start | bytes 393220
  51.9 18.1 %collective-permute-start.11 = (f32[8,4,3,8,128]{4,3,2,1,0:T(8,128)S(1)}, f32[8,4,3,8,128]{4,3,2,1,0:T(8,128)S(1)}, u32[]{:S(2)}, u32[]{:S(2)}) collective-permute-start(f32[8,4,3,8,128]{4,3,2,1,0:T(8,128)S(1)} %slice.9.refs_3_), channel_id=1, source_target_pairs={{0,128},{4,132},{8,136},{12,140},{16,144},{20,148},{24,152},{28,15... | collective-permute-start | bytes 1179656 | tf_op jit(solution)/shard_map/ppermute | solution.py:292
  52.4 20.4 %collective-permute-start.10 = (f32[8,4,3,8,128]{4,3,2,1,0:T(8,128)S(1)}, f32[8,4,3,8,128]{4,3,2,1,0:T(8,128)S(1)}, u32[]{:S(2)}, u32[]{:S(2)}) collective-permute-start(f32[8,4,3,8,128]{4,3,2,1,0:T(8,128)S(1)} %slice.9.refs_3_), channel_id=1, source_target_pairs={{0,64},{4,68},{8,72},{12,76},{16,80},{20,84},{24,88},{28,92},{32,9... | collective-permute-start | bytes 1179656 | tf_op jit(solution)/shard_map/ppermute | solution.py:292
  65.7 19.9 %copy-start.6 = (f32[1024,128]{1,0:T(8,128)}, f32[1024,128]{1,0:T(8,128)S(1)}, u32[]{:S(2)}) copy-start(f32[1024,128]{1,0:T(8,128)S(1)} %collective-permute-done.21.refs_17_) | copy-start | bytes 1572868
  65.7 19.9 %collective-permute-start.22 = (f32[1024,128]{1,0:T(8,128)S(1)}, f32[1024,128]{1,0:T(8,128)S(1)}, u32[]{:S(2)}, u32[]{:S(2)}) collective-permute-start(f32[1024,128]{1,0:T(8,128)S(1)} %collective-permute-done.21.refs_17_), channel_id=1, source_target_pairs={{0,3},{1,0},{2,1},{3,2},{4,7},{5,4},{6,5},{7,6},{8,11},{9,8},{10,9... | collective-permute-start | bytes 1572872 | tf_op jit(solution)/shard_map/ppermute | solution.py:282
  68.4 17.2 %copy-start.7 = (f32[1024,128]{1,0:T(8,128)}, f32[1024,128]{1,0:T(8,128)S(1)}, u32[]{:S(2)}) copy-start(f32[1024,128]{1,0:T(8,128)S(1)} %collective-permute-done.19.refs_14_) | copy-start | bytes 1572868
  68.4 17.3 %collective-permute-start.13 = (f32[8,4,3,8,128]{4,3,2,1,0:T(8,128)S(1)}, f32[8,4,3,8,128]{4,3,2,1,0:T(8,128)S(1)}, u32[]{:S(2)}, u32[]{:S(2)}) collective-permute-start(f32[8,4,3,8,128]{4,3,2,1,0:T(8,128)S(1)} %slice.9.refs_3_), channel_id=1, source_target_pairs={{0,4},{4,0},{8,12},{12,8},{16,20},{20,16},{24,28},{28,24},{32,36},... | collective-permute-start | bytes 1179656 | tf_op jit(solution)/shard_map/ppermute | solution.py:292
  69.9 15.7 %copy-start.9 = (f32[8,4,3,8,128]{4,3,2,1,0:T(8,128)}, f32[8,4,3,8,128]{4,3,2,1,0:T(8,128)S(1)}, u32[]{:S(2)}) copy-start(f32[8,4,3,8,128]{4,3,2,1,0:T(8,128)S(1)} %collective-permute-done.12.refs_6_) | copy-start | bytes 1179652
  69.9 15.8 %collective-permute-start.16 = (f32[8,4,3,8,128]{4,3,2,1,0:T(8,128)S(1)}, f32[8,4,3,8,128]{4,3,2,1,0:T(8,128)S(1)}, u32[]{:S(2)}, u32[]{:S(2)}) collective-permute-start(f32[8,4,3,8,128]{4,3,2,1,0:T(8,128)S(1)} %collective-permute-done.12.refs_6_), channel_id=1, source_target_pairs={{0,4},{4,0},{8,12},{12,8},{16,20},{20,16},{24,28},{28,24},{32,36},... | collective-permute-start | bytes 1179656 | tf_op jit(solution)/shard_map/ppermute | solution.py:292
  70.0 15.6 %copy-start.10 = (f32[8,4,3,8,128]{4,3,2,1,0:T(8,128)}, f32[8,4,3,8,128]{4,3,2,1,0:T(8,128)S(1)}, u32[]{:S(2)}) copy-start(f32[8,4,3,8,128]{4,3,2,1,0:T(8,128)S(1)} %collective-permute-done.11.refs_5_) | copy-start | bytes 1179652
  70.0 15.7 %collective-permute-start.15 = (f32[8,4,3,8,128]{4,3,2,1,0:T(8,128)S(1)}, f32[8,4,3,8,128]{4,3,2,1,0:T(8,128)S(1)}, u32[]{:S(2)}, u32[]{:S(2)}) collective-permute-start(f32[8,4,3,8,128]{4,3,2,1,0:T(8,128)S(1)} %collective-permute-done.11.refs_5_), channel_id=1, source_target_pairs={{0,4},{4,0},{8,12},{12,8},{16,20},{20,16},{24,28},{28,24},{32,36},... | collective-permute-start | bytes 1179656 | tf_op jit(solution)/shard_map/ppermute | solution.py:292
  72.9 12.7 %copy-start.11 = (f32[8,4,3,8,128]{4,3,2,1,0:T(8,128)}, f32[8,4,3,8,128]{4,3,2,1,0:T(8,128)S(1)}, u32[]{:S(2)}) copy-start(f32[8,4,3,8,128]{4,3,2,1,0:T(8,128)S(1)} %collective-permute-done.10.refs_4_) | copy-start | bytes 1179652
  72.9 12.8 %collective-permute-start.14 = (f32[8,4,3,8,128]{4,3,2,1,0:T(8,128)S(1)}, f32[8,4,3,8,128]{4,3,2,1,0:T(8,128)S(1)}, u32[]{:S(2)}, u32[]{:S(2)}) collective-permute-start(f32[8,4,3,8,128]{4,3,2,1,0:T(8,128)S(1)} %collective-permute-done.10.refs_4_), channel_id=1, source_target_pairs={{0,4},{4,0},{8,12},{12,8},{16,20},{20,16},{24,28},{28,24},{32,36},... | collective-permute-start | bytes 1179656 | tf_op jit(solution)/shard_map/ppermute | solution.py:292
  85.6 0.8 copy-start.8
  85.6 0.9 copy-start.12
  85.7 1.0 copy-start.13
  85.7 1.2 %copy-start.14 = (f32[8,4,3,8,128]{4,3,2,1,0:T(8,128)}, f32[8,4,3,8,128]{4,3,2,1,0:T(8,128)S(1)}, u32[]{:S(2)}) copy-start(f32[8,4,3,8,128]{4,3,2,1,0:T(8,128)S(1)} %collective-permute-done.15.refs_9_) | copy-start | bytes 1179652
  85.7 1.3 %copy-start.15 = (f32[8,4,3,8,128]{4,3,2,1,0:T(8,128)}, f32[8,4,3,8,128]{4,3,2,1,0:T(8,128)S(1)}, u32[]{:S(2)}) copy-start(f32[8,4,3,8,128]{4,3,2,1,0:T(8,128)S(1)} %collective-permute-done.14.refs_8_) | copy-start | bytes 1179652

commit v2 on v1

--- a/solution.py
+++ b/solution.py
@@ -118,18 +118,19 @@
     w_ref[b:c, b:c] = w_ref[b:c, b:c] - exact_nt(l21, l21)
 
 
-def factor_blocks(w_ref, l_ref, x_ref):
+def factor_one(w_ref, l_ref, x_ref, block):
     ri = lax.broadcasted_iota(jnp.int32, (BLOCK, BLOCK), 0)
     ci = lax.broadcasted_iota(jnp.int32, (BLOCK, BLOCK), 1)
     eye = jnp.where(ri == ci, 1.0, 0.0).astype(F32)
-
+    cut = lambda v: [v[8 * b : 8 * b + 8] for b in range(GROUPS)]
+    upper, inverse = factor_block(cut(w_ref[block, block]), cut(eye))
+    l_ref[block, block] = jnp.where(ri >= ci, jnp.concatenate(upper, axis=0).T, 0.0)
+    x_ref[block, block] = jnp.where(ri >= ci, jnp.concatenate(inverse, axis=0), 0.0)
+
+
+def factor_two(w_ref, l_ref, x_ref):
     def step(j, carry):
-        block = pl.ds(pl.multiple_of(j * BLOCK, BLOCK), BLOCK)
-        d = w_ref[block, block]
-        cut = lambda v: [v[8 * b : 8 * b + 8] for b in range(GROUPS)]
-        upper, inverse = factor_block(cut(d), cut(eye))
-        l_ref[block, block] = jnp.where(ri >= ci, jnp.concatenate(upper, axis=0).T, 0.0)
-        x_ref[block, block] = jnp.where(ri >= ci, jnp.concatenate(inverse, axis=0), 0.0)
+        factor_one(w_ref, l_ref, x_ref, pl.ds(pl.multiple_of(j * BLOCK, BLOCK), BLOCK))
 
         @pl.when(j == 0)
         def _():
@@ -159,27 +160,31 @@
                     out_ref[rows, lanes[s_y]] = piece[(z, s_y) + at_tile]
 
 
-def first_half(*refs):
+def first_blocks(*refs):
     at_ref, pieces = refs[0], refs[1:9]
-    w_out, l_ref, x_ref, w_ref = refs[9:]
+    w22, l_ref, x_ref, l22, x22, w_ref = refs[10:]
     spread(at_ref, pieces, (), w_ref)
     l_ref[...] = jnp.zeros((PIVOT, HALF), F32)
     x_ref[...] = jnp.zeros((HALF, HALF), F32)
-    factor_blocks(w_ref, l_ref, x_ref)
+    l22[...] = jnp.zeros((HALF, HALF), F32)
+    x22[...] = jnp.zeros((HALF, HALF), F32)
+    factor_two(w_ref, l_ref, x_ref)
     a = slice(0, HALF)
     b = slice(HALF, PIVOT)
     l21 = exact_nt(w_ref[b, a], x_ref[...])
     l_ref[b, :] = l21
-    w_out[...] = w_ref[b, b] - exact_nt(l21, l21)
-
-
-def second_half(w_in, l_in, x_in, l_ref, x_ref, w_ref, l22, x22):
+    w22[...] = w_ref[b, b] - exact_nt(l21, l21)
+    factor_one(w22, l22, x22, slice(0, BLOCK))
+    forward(w22, l22, x22, 0, BLOCK)
+
+
+def last_block(w22, l_in, x_in, l22_in, x22_in, l_ref, x_ref, l22, x22):
     a = slice(0, HALF)
     b = slice(HALF, PIVOT)
-    w_ref[...] = w_in[...]
-    l22[...] = jnp.zeros((HALF, HALF), F32)
-    x22[...] = jnp.zeros((HALF, HALF), F32)
-    factor_blocks(w_ref, l22, x22)
+    l22[...] = l22_in[...]
+    x22[...] = x22_in[...]
+    factor_one(w22, l22, x22, slice(BLOCK, HALF))
+    merge(l22, x22, 0, BLOCK)
     l_ref[:, a] = l_in[...]
     l_ref[a, b] = jnp.zeros((HALF, HALF), F32)
     l_ref[b, b] = l22[...]
@@ -318,6 +323,7 @@
     narrow = pl.BlockSpec((tile, 128), lambda i: (i, 0))
     broad = pl.BlockSpec((tile, local_strip), lambda i: (i, 0))
     corner = pl.BlockSpec((8, 128), lambda i: (0, 0))
+    stacked = lambda which: pl.BlockSpec((None, tile, 128), lambda i: (which, i, 0))
     square = pltpu.VMEM((PIVOT, PIVOT), F32)
     split_square = pltpu.VMEM((2, PIVOT, PIVOT), BF16)
     return pl.pallas_call(
@@ -332,7 +338,9 @@
             matrix(local_rows, local_strip),
             matrix(local_rows, local_strip),
         ),
-        in_specs=[smem_spec()] + [vmem_spec()] * 10 + [narrow] * 8 + [broad] * 2,
+        in_specs=[smem_spec()] + [vmem_spec()] * 10 + [narrow, *[stacked(0)] * 3]
+        + [narrow, *[stacked(1)] * 3]
+        + [broad] * 2,
         out_specs=(corner, corner, narrow, narrow, broad, broad),
         scratch_shapes=[
             square,
@@ -374,34 +382,33 @@
     own_core = [rest] + [along_x_core(rest, s, 0) for s in range(1, N_X)]
     rest_pieces = own_core + [along_x_core(v, 0, 1) for v in own_core]
 
-    def around(value, forward_first):
-        left, right = along_y(value, 1), along_y(value, 3)
-        far = along_y(left, 1) if forward_first else along_y(right, 3)
-        return [value, left, right, far]
-
-    parts = around(panel_block, True)
-    tangent_parts = around(panel_tangent, False)
-
-    w22, l_left, x_first = pl.pallas_call(
-        first_half,
-        name="first_half",
-        out_shape=(matrix(HALF, HALF), matrix(PIVOT, HALF), matrix(HALF, HALF)),
-        in_specs=[smem_spec()] + [vmem_spec()] * 8,
-        out_specs=[vmem_spec()] * 3,
+    both = jnp.stack([panel_block, panel_tangent])
+    left, right = along_y(both, 1), along_y(both, 3)
+    far = along_y(left, 1)
+    parts = [panel_block, left, right, far]
+    tangent_parts = [panel_tangent, left, right, far]
+
+    quarter = matrix(HALF, HALF)
+    factored = pl.pallas_call(
+        first_blocks,
+        name="first_blocks",
+        out_shape=(quarter, matrix(PIVOT, HALF), quarter, quarter, quarter),
+        in_specs=[smem_spec()] + [vmem_spec()] * 8 + [pl.BlockSpec(memory_space=pl.ANY)],
+        out_specs=[vmem_spec()] * 5,
         scratch_shapes=[pltpu.VMEM((PIVOT, PIVOT), F32)],
         compiler_params=LIMIT,
-        cost_estimate=pl.CostEstimate(flops=16 * 10**9, bytes_accessed=10**6, transcendentals=0),
-    )(at, *pivot_pieces)
+        cost_estimate=pl.CostEstimate(flops=22 * 10**9, bytes_accessed=10**6, transcendentals=0),
+    )(at, *pivot_pieces, right)
     whole_factor, inverse = pl.pallas_call(
-        second_half,
-        name="second_half",
+        last_block,
+        name="last_block",
         out_shape=(matrix(PIVOT, PIVOT), matrix(PIVOT, PIVOT)),
-        in_specs=[vmem_spec()] * 3,
+        in_specs=[vmem_spec()] * 5,
         out_specs=[vmem_spec()] * 2,
-        scratch_shapes=[pltpu.VMEM((HALF, HALF), F32)] * 3,
+        scratch_shapes=[pltpu.VMEM((HALF, HALF), F32)] * 2,
         compiler_params=LIMIT,
-        cost_estimate=pl.CostEstimate(flops=16 * 10**9, bytes_accessed=10**6, transcendentals=0),
-    )(w22, l_left, x_first)
+        cost_estimate=pl.CostEstimate(flops=10 * 10**9, bytes_accessed=10**6, transcendentals=0),
+    )(*factored)
 
     return run_panel(
         at, whole_factor, inverse, rest_pieces, parts, tangent_parts, strip_block, strip_tangent

time: 109 us -> 103 us (0.945)
  starting transfers between devices: 39.7 us -> 30.1 us
  waiting for transfers between devices: 16.8 us -> 20.9 us
    ppermute x14, starting transfers between devices: 18.3 us -> 13.3 us  [along_x_core(): return lax.ppermute(value, 'row', pairs)]
    ppermute x9 -> x6, waiting for transfers between devices: 1.83 us -> 6.65 us  [along_y(): return lax.ppermute(value, 'col', [(c, (c + s) % N_Y) for c in range(N_Y)])]
    ppermute x9 -> x6, starting transfers between devices: 13.2 us -> 8.56 us  [along_y(): return lax.ppermute(value, 'col', [(c, (c + s) % N_Y) for c in range(N_Y)])]
  transfers between devices with their start and end apart: 24 -> 21, of which waited for: 4 -> 5; matrix products, arithmetic and copies ran while one was open for 1% -> 1% of each run, Pallas kernels for 23% -> 24%
where the time goes in v2:
time: 103 us; the launch traced here: 102 us
  Pallas kernels  45.6 us (44%)
  starting transfers between devices  30.1 us (29%)
  waiting for transfers between devices  20.9 us (20%)
  local copies, waits for them, and re-layouts  3.35 us (3%)
  other arithmetic  1.4 us (1%)
  between operations  1.12 us (1%)
    pallas_call x1, Pallas kernels, run_panel(): pl.pallas_call(panel, name='panel', grid=(local_rows // tile,), out_shape...  21.3 us
    pallas_call x1, Pallas kernels, body(): pl.pallas_call(first_blocks, name='first_blocks', out_shape=(quarter, mat...  16.6 us
    ppermute x14, starting transfers between devices, along_x_core(): return lax.ppermute(value, 'row', pairs)  13.3 us
    all_to_all x1, waiting for transfers between devices, gather_z(): return lax.all_to_all(spread, 'row', 0, 0, axis_index_groups=ALONG_Z)  12.3 us
    ppermute x6, starting transfers between devices, along_y(): return lax.ppermute(value, 'col', [(c, (c + s) % N_Y) for c in range(N_Y)])  8.56 us
    all_to_all x1, starting transfers between devices, gather_z(): return lax.all_to_all(spread, 'row', 0, 0, axis_index_groups=ALONG_Z)  8.19 us
    pallas_call x1, Pallas kernels, body(): pl.pallas_call(last_block, name='last_block', out_shape=(matrix(PIVOT, PI...  7.6 us
    ppermute x6, waiting for transfers between devices, along_y(): return lax.ppermute(value, 'col', [(c, (c + s) % N_Y) for c in range(N_Y)])  6.65 us
  transfers between devices with their start and end apart: 21, of which 5 were waited for; matrix products, arithmetic and copies ran while one was open for 1% of the time, Pallas kernels for 24%

profile of v2, /device:TPU:1, one launch (start us, length us, event | category | flops | bytes accessed | tf_op | source)
XLA Modules:
  0.0 102.4 jit_solution(14043781956391026192)
XLA Ops:
  0.6 0.0 copy-start
  0.6 0.0 copy-start.1
  0.7 0.9 dynamic-slice_bitcast_fusion.6
  1.6 0.7 maximum_bitcast_fusion
  2.3 2.1 %collective-permute-start = (f32[4,8,128]{2,1,0:T(8,128)S(1)}, f32[4,8,128]{2,1,0:T(8,128)S(1)}, u32[]{:S(2)}, u32[]{:S(2)}) collective-permute-start(f32[4,8,128]{2,1,0:T(8,128)S(1)} %get-tuple-element.29), channel_id=1, source_target_pairs={{0,1},{1,2},{2,3},{3,0},{4,5},{5,6},{6,7},{7,4},{8,9},{9,10},{10,1... | collective-permute-start | bytes 49160 | tf_op jit(solution)/shard_map/ppermute | solution.py:287
  4.4 2.6 %collective-permute-start.1 = (f32[4,8,128]{2,1,0:T(8,128)S(1)}, f32[4,8,128]{2,1,0:T(8,128)S(1)}, u32[]{:S(2)}, u32[]{:S(2)}) collective-permute-start(f32[4,8,128]{2,1,0:T(8,128)S(1)} %get-tuple-element.30), channel_id=1, source_target_pairs={{0,2},{1,3},{2,0},{3,1},{4,6},{5,7},{6,4},{7,5},{8,10},{9,11},{10,... | collective-permute-start | bytes 49160 | tf_op jit(solution)/shard_map/ppermute | solution.py:287
  7.0 1.1 %collective-permute-start.2 = (f32[4,8,128]{2,1,0:T(8,128)S(1)}, f32[4,8,128]{2,1,0:T(8,128)S(1)}, u32[]{:S(2)}, u32[]{:S(2)}) collective-permute-start(f32[4,8,128]{2,1,0:T(8,128)S(1)} %get-tuple-element.31), channel_id=1, source_target_pairs={{0,3},{1,0},{2,1},{3,2},{4,7},{5,4},{6,5},{7,6},{8,11},{9,8},{10,9... | collective-permute-start | bytes 49160 | tf_op jit(solution)/shard_map/ppermute | solution.py:287
  8.1 0.4 collective-permute-done.1
  8.5 1.4 %collective-permute-done.2 = f32[4,8,128]{2,1,0:T(8,128)S(1)} collective-permute-done((f32[4,8,128]{2,1,0:T(8,128)S(1)}, f32[4,8,128]{2,1,0:T(8,128)S(1)}, u32[]{:S(2)}, u32[]{:S(2)}) %collective-permute-start.2) | collective-permute-done | bytes 16416 | tf_op jit(solution)/shard_map/ppermute | solution.py:287
  9.9 0.9 broadcast_in_dim.2
  10.8 8.2 %all-to-all-start = ((f32[8,4,4,8,128]{4,3,2,1,0:T(8,128)}), f32[8,4,4,8,128]{4,3,2,1,0:T(8,128)S(1)}, u32[]{:S(2)}, u32[]{:S(2)}) async-start(f32[8,4,4,8,128]{4,3,2,1,0:T(8,128)} %broadcast_in_dim.2), calls=%async_computation | async-start | bytes 1048576 | tf_op jit(solution)/shard_map/all_to_all | solution.py:302
  19.0 0.1 pad_maximum_fusion
  19.0 0.1 collective-permute-start.18
  19.1 2.7 %collective-permute-start.10 = (f32[2,1024,128]{2,1,0:T(8,128)S(1)}, f32[2,1024,128]{2,1,0:T(8,128)}, u32[]{:S(2)}, u32[]{:S(2)}) collective-permute-start(f32[2,1024,128]{2,1,0:T(8,128)S(1)} %pad_maximum_fusion), channel_id=1, source_target_pairs={{0,3},{1,0},{2,1},{3,2},{4,7},{5,4},{6,5},{7,6},{8,11},{9,8},{10,9... | collective-permute-start | bytes 3145736 | tf_op jit(solution)/shard_map/ppermute | solution.py:287
  21.8 12.3 %all-to-all-done = f32[8,4,4,8,128]{4,3,2,1,0:T(8,128)S(1)} async-done(((f32[8,4,4,8,128]{4,3,2,1,0:T(8,128)}), f32[8,4,4,8,128]{4,3,2,1,0:T(8,128)S(1)}, u32[]{:S(2)}, u32[]{:S(2)}) %all-to-all-start) | async-done | bytes 524320 | tf_op jit(solution)/shard_map/all_to_all | solution.py:302
  34.1 2.6 %collective-permute-start.5 = (f32[8,4,8,128]{3,2,1,0:T(8,128)S(1)}, f32[8,4,8,128]{3,2,1,0:T(8,128)S(1)}, u32[]{:S(2)}, u32[]{:S(2)}) collective-permute-start(f32[8,4,8,128]{3,2,1,0:T(8,128)S(1)} %slice_bitcast_fusion.refs_1_), channel_id=1, source_target_pairs={{0,192},{4,196},{8,200},{12,204},{16,208},{20,212},{24,216},{28,22... | collective-permute-start | bytes 393224 | tf_op jit(solution)/shard_map/ppermute | solution.py:297
  36.7 0.5 collective-permute-start.4
  37.2 0.6 collective-permute-start.3
  37.8 4.8 %collective-permute-done.18.refs_12_.refs_16_ = f32[2,1024,128]{2,1,0:T(8,128)S(1)} collective-permute-done((f32[2,1024,128]{2,1,0:T(8,128)S(1)}, f32[2,1024,128]{2,1,0:T(8,128)S(1)}, u32[]{:S(2)}, u32[]{:S(2)}) %collective-permute-start.18) | collective-permute-done | bytes 1048608 | tf_op jit(solution)/shard_map/ppermute | solution.py:287
  42.6 3.3 %collective-permute-start.6 = (f32[8,4,8,128]{3,2,1,0:T(8,128)S(1)}, f32[8,4,8,128]{3,2,1,0:T(8,128)S(1)}, u32[]{:S(2)}, u32[]{:S(2)}) collective-permute-start(f32[8,4,8,128]{3,2,1,0:T(8,128)S(1)} %slice_bitcast_fusion.refs_1_), channel_id=1, source_target_pairs={{0,4},{4,0},{8,12},{12,8},{16,20},{20,16},{24,28},{28,24},{32,36},... | collective-permute-start | bytes 393224 | tf_op jit(solution)/shard_map/ppermute | solution.py:297
  45.9 0.0 collective-permute-done.5.refs_4_
  45.9 0.1 collective-permute-start.9
  46.0 0.8 collective-permute-start.8
  46.8 0.0 collective-permute-done.3.refs_2_
  46.8 1.3 %collective-permute-start.7 = (f32[8,4,8,128]{3,2,1,0:T(8,128)S(1)}, f32[8,4,8,128]{3,2,1,0:T(8,128)}, u32[]{:S(2)}, u32[]{:S(2)}) collective-permute-start(f32[8,4,8,128]{3,2,1,0:T(8,128)S(1)} %collective-permute-done.3.refs_2_), channel_id=1, source_target_pairs={{0,4},{4,0},{8,12},{12,8},{16,20},{20,16},{24,28},{28,24},{32,36},... | collective-permute-start | bytes 393224 | tf_op jit(solution)/shard_map/ppermute | solution.py:297
  48.1 0.6 pad_add_fusion.refs_0_
  48.8 0.0 collective-permute-done.10.refs_9_.refs_13_.refs_17_
  48.8 0.1 collective-permute-start.14
  48.9 0.0 collective-permute-done.6.refs_5_
  49.0 1.3 %collective-permute-start.13 = (f32[8,4,3,8,128]{4,3,2,1,0:T(8,128)S(1)}, f32[8,4,3,8,128]{4,3,2,1,0:T(8,128)S(1)}, u32[]{:S(2)}, u32[]{:S(2)}) collective-permute-start(f32[8,4,3,8,128]{4,3,2,1,0:T(8,128)S(1)} %slice.9.refs_3_), channel_id=1, source_target_pairs={{0,192},{4,196},{8,200},{12,204},{16,208},{20,212},{24,216},{28,22... | collective-permute-start | bytes 1179656 | tf_op jit(solution)/shard_map/ppermute | solution.py:297
  50.2 0.5 collective-permute-start.12
  50.8 0.6 collective-permute-start.11
  51.4 0.0 collective-permute-start.19
  51.4 16.6 %first_blocks.1 = (f32[256,256]{1,0:T(8,128)}, f32[512,256]{1,0:T(8,128)}, f32[256,256]{1,0:T(8,128)}, f32[256,256]{1,0:T(8,128)}, f32[256,256]{1,0:T(8,128)}) custom-call(s32[4]{0:T(128)} %pad_add_fusion.refs_0_, f32[8,4,8,128]{3,2,1,0:T(8,128)} %copy-done.3, f32[8,4,8,128]{3,2,1,0:T(8,128)} %copy-done.15, f32[8,4,8,128]{3,2,1,0:T(8,128)} %copy-done.14, ...), custom_call_target="tpu_custom_call" | custom-call | flops 22000001024 | bytes 1000000 | tf_op jit(solution)/shard_map/first_blocks/pallas_call | solution.py:392
  68.1 1.0 collective-permute-start.17
  69.1 0.1 collective-permute-start.16
  69.2 2.0 %collective-permute-done.11.refs_4_ = f32[8,4,3,8,128]{4,3,2,1,0:T(8,128)S(1)} collective-permute-done((f32[8,4,3,8,128]{4,3,2,1,0:T(8,128)S(1)}, f32[8,4,3,8,128]{4,3,2,1,0:T(8,128)S(1)}, u32[]{:S(2)}, u32[]{:S(2)}) %collective-permute-start.11) | collective-permute-done | bytes 393248 | tf_op jit(solution)/shard_map/ppermute | solution.py:297
  71.2 0.5 collective-permute-start.15
  71.7 7.6 %last_block.1 = (f32[512,512]{1,0:T(8,128)}, f32[512,512]{1,0:T(8,128)}) custom-call(f32[256,256]{1,0:T(8,128)} %get-tuple-element.13.w22, f32[512,256]{1,0:T(8,128)} %get-tuple-element.14.l_in, f32[256,256]{1,0:T(8,128)} %get-tuple-element.15.x_in, f32[256,256]{1,0:T(8,128)} %get-tuple-element.16.l22_in, f32[256,256]{1,0:T(8,128)} %get-tuple-element.17.x22_in), custom_call_target="tpu_custom_call" | custom-call | flops 10000000000 | bytes 1000000 | tf_op jit(solution)/shard_map/last_block/pallas_call | solution.py:402
  79.3 0.0 collective-permute-done.14.refs_7_
  79.3 0.0 collective-permute-done.17.refs_10_
  79.4 0.0 collective-permute-done.15.refs_8_
  79.4 0.6 copy-done.6
  80.1 0.2 copy-done.10
  80.2 0.2 copy-done.11
  80.4 0.2 copy-done.12
  80.6 0.3 copy-done.5
  80.9 21.3 %panel.1 = (f32[8,128]{1,0:T(8,128)}, f32[8,128]{1,0:T(8,128)}, f32[1024,128]{1,0:T(8,128)}, f32[1024,128]{1,0:T(8,128)}, f32[1024,512]{1,0:T(8,128)}, /*index=5*/f32[1024,512]{1,0:T(8,128)}) custom-call(s32[4]{0:T(128)} %pad_add_fusion.refs_0_, f32[512,512]{1,0:T(8,128)} %get-tuple-element.18.refs_1_, f32[512,512]{1,0:T(8,128)} %get-tuple-element.19.refs_2_, ...), custom_call_target="tpu_custom_call" | custom-call | flops 10000000000 | bytes 20000000 | tf_op jit(solution)/shard_map/panel/pallas_call | solution.py:329
  (43 shorter events, 0.1 us)
Async XLA Ops:
  0.6 18.3 %copy-start = (f32[1024,128]{1,0:T(8,128)S(1)}, f32[1024,128]{1,0:T(8,128)}, u32[]{:S(2)}) copy-start(f32[1024,128]{1,0:T(8,128)} %refs_15_.1) | copy-start | bytes 1572868
  0.6 18.3 %copy-start.1 = (f32[1024,128]{1,0:T(8,128)S(1)}, f32[1024,128]{1,0:T(8,128)}, u32[]{:S(2)}) copy-start(f32[1024,128]{1,0:T(8,128)} %refs_11_.1) | copy-start | bytes 1572868
  2.3 5.8 %collective-permute-start = (f32[4,8,128]{2,1,0:T(8,128)S(1)}, f32[4,8,128]{2,1,0:T(8,128)S(1)}, u32[]{:S(2)}, u32[]{:S(2)}) collective-permute-start(f32[4,8,128]{2,1,0:T(8,128)S(1)} %get-tuple-element.29), channel_id=1, source_target_pairs={{0,1},{1,2},{2,3},{3,0},{4,5},{5,6},{6,7},{7,4},{8,9},{9,10},{10,1... | collective-permute-start | bytes 49160 | tf_op jit(solution)/shard_map/ppermute | solution.py:287
  4.4 4.1 %collective-permute-start.1 = (f32[4,8,128]{2,1,0:T(8,128)S(1)}, f32[4,8,128]{2,1,0:T(8,128)S(1)}, u32[]{:S(2)}, u32[]{:S(2)}) collective-permute-start(f32[4,8,128]{2,1,0:T(8,128)S(1)} %get-tuple-element.30), channel_id=1, source_target_pairs={{0,2},{1,3},{2,0},{3,1},{4,6},{5,7},{6,4},{7,5},{8,10},{9,11},{10,... | collective-permute-start | bytes 49160 | tf_op jit(solution)/shard_map/ppermute | solution.py:287
  7.0 2.9 %collective-permute-start.2 = (f32[4,8,128]{2,1,0:T(8,128)S(1)}, f32[4,8,128]{2,1,0:T(8,128)S(1)}, u32[]{:S(2)}, u32[]{:S(2)}) collective-permute-start(f32[4,8,128]{2,1,0:T(8,128)S(1)} %get-tuple-element.31), channel_id=1, source_target_pairs={{0,3},{1,0},{2,1},{3,2},{4,7},{5,4},{6,5},{7,6},{8,11},{9,8},{10,9... | collective-permute-start | bytes 49160 | tf_op jit(solution)/shard_map/ppermute | solution.py:287
  10.8 23.3 %all-to-all-start = ((f32[8,4,4,8,128]{4,3,2,1,0:T(8,128)}), f32[8,4,4,8,128]{4,3,2,1,0:T(8,128)S(1)}, u32[]{:S(2)}, u32[]{:S(2)}) async-start(f32[8,4,4,8,128]{4,3,2,1,0:T(8,128)} %broadcast_in_dim.2), calls=%async_computation | async-start | bytes 1048576 | tf_op jit(solution)/shard_map/all_to_all | solution.py:302
  19.0 23.6 %collective-permute-start.18 = (f32[2,1024,128]{2,1,0:T(8,128)S(1)}, f32[2,1024,128]{2,1,0:T(8,128)S(1)}, u32[]{:S(2)}, u32[]{:S(2)}) collective-permute-start(f32[2,1024,128]{2,1,0:T(8,128)S(1)} %pad_maximum_fusion), channel_id=1, source_target_pairs={{0,1},{1,2},{2,3},{3,0},{4,5},{5,6},{6,7},{7,4},{8,9},{9,10},{10,1... | collective-permute-start | bytes 3145736 | tf_op jit(solution)/shard_map/ppermute | solution.py:287
  19.1 29.7 %collective-permute-start.10 = (f32[2,1024,128]{2,1,0:T(8,128)S(1)}, f32[2,1024,128]{2,1,0:T(8,128)}, u32[]{:S(2)}, u32[]{:S(2)}) collective-permute-start(f32[2,1024,128]{2,1,0:T(8,128)S(1)} %pad_maximum_fusion), channel_id=1, source_target_pairs={{0,3},{1,0},{2,1},{3,2},{4,7},{5,4},{6,5},{7,6},{8,11},{9,8},{10,9... | collective-permute-start | bytes 3145736 | tf_op jit(solution)/shard_map/ppermute | solution.py:287
  34.1 17.3 %copy-start.3 = (f32[8,4,8,128]{3,2,1,0:T(8,128)}, f32[8,4,8,128]{3,2,1,0:T(8,128)S(1)}, u32[]{:S(2)}) copy-start(f32[8,4,8,128]{3,2,1,0:T(8,128)S(1)} %slice_bitcast_fusion.refs_1_) | copy-start | bytes 393220
  34.1 11.8 %collective-permute-start.5 = (f32[8,4,8,128]{3,2,1,0:T(8,128)S(1)}, f32[8,4,8,128]{3,2,1,0:T(8,128)S(1)}, u32[]{:S(2)}, u32[]{:S(2)}) collective-permute-start(f32[8,4,8,128]{3,2,1,0:T(8,128)S(1)} %slice_bitcast_fusion.refs_1_), channel_id=1, source_target_pairs={{0,192},{4,196},{8,200},{12,204},{16,208},{20,212},{24,216},{28,22... | collective-permute-start | bytes 393224 | tf_op jit(solution)/shard_map/ppermute | solution.py:297
  36.7 9.4 %collective-permute-start.4 = (f32[8,4,8,128]{3,2,1,0:T(8,128)S(1)}, f32[8,4,8,128]{3,2,1,0:T(8,128)S(1)}, u32[]{:S(2)}, u32[]{:S(2)}) collective-permute-start(f32[8,4,8,128]{3,2,1,0:T(8,128)S(1)} %slice_bitcast_fusion.refs_1_), channel_id=1, source_target_pairs={{0,128},{4,132},{8,136},{12,140},{16,144},{20,148},{24,152},{28,15... | collective-permute-start | bytes 393224 | tf_op jit(solution)/shard_map/ppermute | solution.py:297
  37.2 9.7 %collective-permute-start.3 = (f32[8,4,8,128]{3,2,1,0:T(8,128)S(1)}, f32[8,4,8,128]{3,2,1,0:T(8,128)S(1)}, u32[]{:S(2)}, u32[]{:S(2)}) collective-permute-start(f32[8,4,8,128]{3,2,1,0:T(8,128)S(1)} %slice_bitcast_fusion.refs_1_), channel_id=1, source_target_pairs={{0,64},{4,68},{8,72},{12,76},{16,80},{20,84},{24,88},{28,92},{32,9... | collective-permute-start | bytes 393224 | tf_op jit(solution)/shard_map/ppermute | solution.py:297
  42.6 25.4 %copy-start.4 = (f32[2,1024,128]{2,1,0:T(8,128)}, f32[2,1024,128]{2,1,0:T(8,128)S(1)}, u32[]{:S(2)}) copy-start(f32[2,1024,128]{2,1,0:T(8,128)S(1)} %collective-permute-done.18.refs_12_.refs_16_) | copy-start | bytes 3145732
  42.6 6.3 %collective-permute-start.6 = (f32[8,4,8,128]{3,2,1,0:T(8,128)S(1)}, f32[8,4,8,128]{3,2,1,0:T(8,128)S(1)}, u32[]{:S(2)}, u32[]{:S(2)}) collective-permute-start(f32[8,4,8,128]{3,2,1,0:T(8,128)S(1)} %slice_bitcast_fusion.refs_1_), channel_id=1, source_target_pairs={{0,4},{4,0},{8,12},{12,8},{16,20},{20,16},{24,28},{28,24},{32,36},... | collective-permute-start | bytes 393224 | tf_op jit(solution)/shard_map/ppermute | solution.py:297
  45.9 5.5 %copy-start.13 = (f32[8,4,8,128]{3,2,1,0:T(8,128)}, f32[8,4,8,128]{3,2,1,0:T(8,128)S(1)}, u32[]{:S(2)}) copy-start(f32[8,4,8,128]{3,2,1,0:T(8,128)S(1)} %collective-permute-done.5.refs_4_) | copy-start | bytes 393220
  45.9 4.3 %collective-permute-start.9 = (f32[8,4,8,128]{3,2,1,0:T(8,128)S(1)}, f32[8,4,8,128]{3,2,1,0:T(8,128)S(1)}, u32[]{:S(2)}, u32[]{:S(2)}) collective-permute-start(f32[8,4,8,128]{3,2,1,0:T(8,128)S(1)} %collective-permute-done.5.refs_4_), channel_id=1, source_target_pairs={{0,4},{4,0},{8,12},{12,8},{16,20},{20,16},{24,28},{28,24},{32,36},... | collective-permute-start | bytes 393224 | tf_op jit(solution)/shard_map/ppermute | solution.py:297
  46.0 5.4 %copy-start.14 = (f32[8,4,8,128]{3,2,1,0:T(8,128)}, f32[8,4,8,128]{3,2,1,0:T(8,128)S(1)}, u32[]{:S(2)}) copy-start(f32[8,4,8,128]{3,2,1,0:T(8,128)S(1)} %collective-permute-done.4.refs_3_) | copy-start | bytes 393220
  46.0 4.7 %collective-permute-start.8 = (f32[8,4,8,128]{3,2,1,0:T(8,128)S(1)}, f32[8,4,8,128]{3,2,1,0:T(8,128)S(1)}, u32[]{:S(2)}, u32[]{:S(2)}) collective-permute-start(f32[8,4,8,128]{3,2,1,0:T(8,128)S(1)} %collective-permute-done.4.refs_3_), channel_id=1, source_target_pairs={{0,4},{4,0},{8,12},{12,8},{16,20},{20,16},{24,28},{28,24},{32,36},... | collective-permute-start | bytes 393224 | tf_op jit(solution)/shard_map/ppermute | solution.py:297
  46.8 4.6 %copy-start.15 = (f32[8,4,8,128]{3,2,1,0:T(8,128)}, f32[8,4,8,128]{3,2,1,0:T(8,128)S(1)}, u32[]{:S(2)}) copy-start(f32[8,4,8,128]{3,2,1,0:T(8,128)S(1)} %collective-permute-done.3.refs_2_) | copy-start | bytes 393220
  46.8 4.5 %collective-permute-start.7 = (f32[8,4,8,128]{3,2,1,0:T(8,128)S(1)}, f32[8,4,8,128]{3,2,1,0:T(8,128)}, u32[]{:S(2)}, u32[]{:S(2)}) collective-permute-start(f32[8,4,8,128]{3,2,1,0:T(8,128)S(1)} %collective-permute-done.3.refs_2_), channel_id=1, source_target_pairs={{0,4},{4,0},{8,12},{12,8},{16,20},{20,16},{24,28},{28,24},{32,36},... | collective-permute-start | bytes 393224 | tf_op jit(solution)/shard_map/ppermute | solution.py:297
  48.8 19.3 %copy-start.2 = (f32[8,4,3,8,128]{4,3,2,1,0:T(8,128)}, f32[8,4,3,8,128]{4,3,2,1,0:T(8,128)S(1)}, u32[]{:S(2)}) copy-start(f32[8,4,3,8,128]{4,3,2,1,0:T(8,128)S(1)} %slice.9.refs_3_) | copy-start | bytes 1179652
  48.8 30.5 %collective-permute-start.14 = (f32[8,4,3,8,128]{4,3,2,1,0:T(8,128)S(1)}, f32[8,4,3,8,128]{4,3,2,1,0:T(8,128)S(1)}, u32[]{:S(2)}, u32[]{:S(2)}) collective-permute-start(f32[8,4,3,8,128]{4,3,2,1,0:T(8,128)S(1)} %slice.9.refs_3_), channel_id=1, source_target_pairs={{0,4},{4,0},{8,12},{12,8},{16,20},{20,16},{24,28},{28,24},{32,36},... | collective-permute-start | bytes 1179656 | tf_op jit(solution)/shard_map/ppermute | solution.py:297
  48.9 2.5 %copy-start.16 = (f32[8,4,8,128]{3,2,1,0:T(8,128)}, f32[8,4,8,128]{3,2,1,0:T(8,128)S(1)}, u32[]{:S(2)}) copy-start(f32[8,4,8,128]{3,2,1,0:T(8,128)S(1)} %collective-permute-done.6.refs_5_) | copy-start | bytes 393220
  49.0 19.1 %collective-permute-start.13 = (f32[8,4,3,8,128]{4,3,2,1,0:T(8,128)S(1)}, f32[8,4,3,8,128]{4,3,2,1,0:T(8,128)S(1)}, u32[]{:S(2)}, u32[]{:S(2)}) collective-permute-start(f32[8,4,3,8,128]{4,3,2,1,0:T(8,128)S(1)} %slice.9.refs_3_), channel_id=1, source_target_pairs={{0,192},{4,196},{8,200},{12,204},{16,208},{20,212},{24,216},{28,22... | collective-permute-start | bytes 1179656 | tf_op jit(solution)/shard_map/ppermute | solution.py:297
  50.2 1.2 %copy-start.17 = (f32[8,4,8,128]{3,2,1,0:T(8,128)}, f32[8,4,8,128]{3,2,1,0:T(8,128)S(1)}, u32[]{:S(2)}) copy-start(f32[8,4,8,128]{3,2,1,0:T(8,128)S(1)} %collective-permute-done.9.refs_8_) | copy-start | bytes 393220
  50.2 18.9 %collective-permute-start.12 = (f32[8,4,3,8,128]{4,3,2,1,0:T(8,128)S(1)}, f32[8,4,3,8,128]{4,3,2,1,0:T(8,128)S(1)}, u32[]{:S(2)}, u32[]{:S(2)}) collective-permute-start(f32[8,4,3,8,128]{4,3,2,1,0:T(8,128)S(1)} %slice.9.refs_3_), channel_id=1, source_target_pairs={{0,128},{4,132},{8,136},{12,140},{16,144},{20,148},{24,152},{28,15... | collective-permute-start | bytes 1179656 | tf_op jit(solution)/shard_map/ppermute | solution.py:297
  50.8 0.7 copy-start.18
  50.8 20.4 %collective-permute-start.11 = (f32[8,4,3,8,128]{4,3,2,1,0:T(8,128)S(1)}, f32[8,4,3,8,128]{4,3,2,1,0:T(8,128)S(1)}, u32[]{:S(2)}, u32[]{:S(2)}) collective-permute-start(f32[8,4,3,8,128]{4,3,2,1,0:T(8,128)S(1)} %slice.9.refs_3_), channel_id=1, source_target_pairs={{0,64},{4,68},{8,72},{12,76},{16,80},{20,84},{24,88},{28,92},{32,9... | collective-permute-start | bytes 1179656 | tf_op jit(solution)/shard_map/ppermute | solution.py:297
  51.4 28.0 %collective-permute-start.19 = (f32[2,1024,128]{2,1,0:T(8,128)S(1)}, f32[2,1024,128]{2,1,0:T(8,128)S(1)}, u32[]{:S(2)}, u32[]{:S(2)}) collective-permute-start(f32[2,1024,128]{2,1,0:T(8,128)S(1)} %collective-permute-done.18.refs_12_.refs_16_), channel_id=1, source_target_pairs={{0,1},{1,2},{2,3},{3,0},{4,5},{5,6},{6,7},{7,4},{8,9},{9,10},{10,1... | collective-permute-start | bytes 3145736 | tf_op jit(solution)/shard_map/ppermute | solution.py:287
  68.1 11.2 %copy-start.7 = (f32[8,4,3,8,128]{4,3,2,1,0:T(8,128)}, f32[8,4,3,8,128]{4,3,2,1,0:T(8,128)S(1)}, u32[]{:S(2)}) copy-start(f32[8,4,3,8,128]{4,3,2,1,0:T(8,128)S(1)} %collective-permute-done.13.refs_6_) | copy-start | bytes 1179652
  68.1 11.2 %collective-permute-start.17 = (f32[8,4,3,8,128]{4,3,2,1,0:T(8,128)S(1)}, f32[8,4,3,8,128]{4,3,2,1,0:T(8,128)S(1)}, u32[]{:S(2)}, u32[]{:S(2)}) collective-permute-start(f32[8,4,3,8,128]{4,3,2,1,0:T(8,128)S(1)} %collective-permute-done.13.refs_6_), channel_id=1, source_target_pairs={{0,4},{4,0},{8,12},{12,8},{16,20},{20,16},{24,28},{28,24},{32,36},... | collective-permute-start | bytes 1179656 | tf_op jit(solution)/shard_map/ppermute | solution.py:297
  69.1 10.2 %copy-start.8 = (f32[8,4,3,8,128]{4,3,2,1,0:T(8,128)}, f32[8,4,3,8,128]{4,3,2,1,0:T(8,128)S(1)}, u32[]{:S(2)}) copy-start(f32[8,4,3,8,128]{4,3,2,1,0:T(8,128)S(1)} %collective-permute-done.12.refs_5_) | copy-start | bytes 1179652
  69.1 10.2 %collective-permute-start.16 = (f32[8,4,3,8,128]{4,3,2,1,0:T(8,128)S(1)}, f32[8,4,3,8,128]{4,3,2,1,0:T(8,128)S(1)}, u32[]{:S(2)}, u32[]{:S(2)}) collective-permute-start(f32[8,4,3,8,128]{4,3,2,1,0:T(8,128)S(1)} %collective-permute-done.12.refs_5_), channel_id=1, source_target_pairs={{0,4},{4,0},{8,12},{12,8},{16,20},{20,16},{24,28},{28,24},{32,36},... | collective-permute-start | bytes 1179656 | tf_op jit(solution)/shard_map/ppermute | solution.py:297
  71.2 8.1 %copy-start.9 = (f32[8,4,3,8,128]{4,3,2,1,0:T(8,128)}, f32[8,4,3,8,128]{4,3,2,1,0:T(8,128)S(1)}, u32[]{:S(2)}) copy-start(f32[8,4,3,8,128]{4,3,2,1,0:T(8,128)S(1)} %collective-permute-done.11.refs_4_) | copy-start | bytes 1179652
  71.2 8.2 %collective-permute-start.15 = (f32[8,4,3,8,128]{4,3,2,1,0:T(8,128)S(1)}, f32[8,4,3,8,128]{4,3,2,1,0:T(8,128)S(1)}, u32[]{:S(2)}, u32[]{:S(2)}) collective-permute-start(f32[8,4,3,8,128]{4,3,2,1,0:T(8,128)S(1)} %collective-permute-done.11.refs_4_), channel_id=1, source_target_pairs={{0,4},{4,0},{8,12},{12,8},{16,20},{20,16},{24,28},{28,24},{32,36},... | collective-permute-start | bytes 1179656 | tf_op jit(solution)/shard_map/ppermute | solution.py:297
  79.3 0.7 copy-start.6
  79.3 0.9 copy-start.10
  79.4 1.0 copy-start.11
  79.4 1.2 %copy-start.12 = (f32[8,4,3,8,128]{4,3,2,1,0:T(8,128)}, f32[8,4,3,8,128]{4,3,2,1,0:T(8,128)S(1)}, u32[]{:S(2)}) copy-start(f32[8,4,3,8,128]{4,3,2,1,0:T(8,128)S(1)} %collective-permute-done.15.refs_8_) | copy-start | bytes 1179652
  79.4 1.5 %copy-start.5 = (f32[2,1024,128]{2,1,0:T(8,128)}, f32[2,1024,128]{2,1,0:T(8,128)S(1)}, u32[]{:S(2)}) copy-start(f32[2,1024,128]{2,1,0:T(8,128)S(1)} %collective-permute-done.19.refs_14_.refs_18_) | copy-start | bytes 3145732

commit v3 on v2

--- a/solution.py
+++ b/solution.py
@@ -51,6 +51,16 @@
     left = jnp.concatenate([a[0], a[0], a[1]], axis=contract[0][0])
     right = jnp.concatenate([b[0], b[1], b[0]], axis=contract[1][0])
     return product(left, right, contract)
+
+
+def end_to_end(a):
+    return jnp.concatenate([a[0], a[0], a[1]], axis=1)
+
+
+def store_stacked(ref, b):
+    depth = b[0].shape[0]
+    for i, half in enumerate((b[0], b[1], b[0])):
+        ref[i * depth : (i + 1) * depth] = half
 
 
 def split_nt(a, b):
@@ -162,12 +172,11 @@
 
 def first_blocks(*refs):
     at_ref, pieces = refs[0], refs[1:9]
-    w22, l_ref, x_ref, l22, x22, w_ref = refs[10:]
+    x_ref, t_ref, own_left, w_last, l_low, x_mid = refs[10:16]
+    w_ref, l_ref, w22, l22, x22 = refs[16:]
     spread(at_ref, pieces, (), w_ref)
     l_ref[...] = jnp.zeros((PIVOT, HALF), F32)
     x_ref[...] = jnp.zeros((HALF, HALF), F32)
-    l22[...] = jnp.zeros((HALF, HALF), F32)
-    x22[...] = jnp.zeros((HALF, HALF), F32)
     factor_two(w_ref, l_ref, x_ref)
     a = slice(0, HALF)
     b = slice(HALF, PIVOT)
@@ -176,27 +185,38 @@
     w22[...] = w_ref[b, b] - exact_nt(l21, l21)
     factor_one(w22, l22, x22, slice(0, BLOCK))
     forward(w22, l22, x22, 0, BLOCK)
-
-
-def last_block(w22, l_in, x_in, l22_in, x22_in, l_ref, x_ref, l22, x22):
-    a = slice(0, HALF)
-    b = slice(HALF, PIVOT)
-    l22[...] = l22_in[...]
-    x22[...] = x22_in[...]
+    t_ref[...] = exact_nn(l_ref[b, :], x_ref[...])
+    own_left[...] = l_ref[pl.ds(pl.multiple_of(at_ref[0] * 8, 8), 8), :]
+    w_last[...] = w22[BLOCK:, BLOCK:]
+    l_low[...] = l22[:, :BLOCK]
+    x_mid[...] = x22[:BLOCK, :BLOCK]
+
+
+def last_block(at_ref, t_in, own_left, w_last, l_low, x_mid, own_ref, x_low, w22, l22, x22):
+    zero = jnp.zeros((BLOCK, BLOCK), F32)
+    w22[BLOCK:, BLOCK:] = w_last[...]
+    l22[:, :BLOCK] = l_low[...]
+    l22[:BLOCK, BLOCK:] = zero
+    x22[:BLOCK, :BLOCK] = x_mid[...]
+    x22[:BLOCK, BLOCK:] = zero
     factor_one(w22, l22, x22, slice(BLOCK, HALF))
     merge(l22, x22, 0, BLOCK)
-    l_ref[:, a] = l_in[...]
-    l_ref[a, b] = jnp.zeros((HALF, HALF), F32)
-    l_ref[b, b] = l22[...]
-    x_ref[a, a] = x_in[...]
-    x_ref[a, b] = jnp.zeros((HALF, HALF), F32)
-    x_ref[b, b] = x22[...]
-    x_ref[b, a] = -exact_nn(x22[...], exact_nn(l_in[b, :], x_in[...]))
-
-
-def times_upper(a, b):
-    left = split_product([v[:, :HALF] for v in a], [v[:HALF, :HALF] for v in b])
-    right = split_product(a, [v[:, HALF:] for v in b])
+    x_low[:, HALF:] = x22[...]
+    x_low[:, :HALF] = -exact_nn(x22[...], t_in[...])
+    row = at_ref[0] * 8 - HALF
+    right = l22[pl.ds(pl.multiple_of(jnp.maximum(row, 0), 8), 8), :]
+    own_ref[:, :HALF] = own_left[...]
+    own_ref[:, HALF:] = jnp.where(row >= 0, right, 0.0)
+
+
+def store_upper(left_ref, right_ref, b):
+    store_stacked(left_ref, [v[:HALF, :HALF] for v in b])
+    store_stacked(right_ref, [v[:, HALF:] for v in b])
+
+
+def times_upper(a, left_ref, right_ref):
+    left = product(end_to_end([v[:, :HALF] for v in a]), left_ref[...], ((1,), (0,)))
+    right = product(end_to_end(a), right_ref[...], ((1,), (0,)))
     return jnp.concatenate([left, right], axis=1)
 
 
@@ -223,12 +243,12 @@
 
 
 def panel(*refs):
-    at_ref, l_ref, x_ref = refs[:3]
-    pieces = refs[3:11]
-    parts, tangent_parts = refs[11:15], refs[15:19]
-    strip_ref, strip_tangent_ref = refs[19:21]
-    factor_out, change_out, panel_out, panel_change_out, strip_out, strip_change_out = refs[21:27]
-    ad, raw, phi, xs, phis, qs, qds, rows_ref, done_ref = refs[27:]
+    at_ref, l_ref, x_first, x_low = refs[:4]
+    pieces = refs[4:12]
+    parts, tangent_parts = refs[12:16], refs[16:20]
+    strip_ref, strip_tangent_ref = refs[20:22]
+    factor_out, change_out, panel_out, panel_change_out, strip_out, strip_change_out = refs[22:28]
+    ad, raw, phi, xs_l, xs_r, phis_l, phis_r, qs, rows_ref, done_ref, x_ref = refs[28:]
     col = at_ref[1]
     whole = slice(None)
 
@@ -237,19 +257,22 @@
         spread(at_ref, pieces, (0,), ad)
         spread(at_ref, pieces, (1,), raw.at[0])
         spread(at_ref, pieces, (2,), raw.at[1])
+        x_ref[:HALF, :HALF] = x_first[...]
+        x_ref[:HALF, HALF:] = jnp.zeros((HALF, HALF), F32)
+        x_ref[HALF:, :] = x_low[...]
         tangent_factor(x_ref, ad, phi)
-        own = pl.ds(pl.multiple_of(at_ref[0] * 8, 8), 8)
         lanes = pl.ds(pl.multiple_of(col * 128, 128), 128)
-        factor_out[...] = l_ref[own, lanes]
-        change_out[...] = exact_nn(l_ref[own, :], phi[:, lanes])
+        factor_out[...] = l_ref[:, lanes]
+        change_out[...] = exact_nn(l_ref[...], phi[:, lanes])
         inverse = halves(x_ref[...])
-        xs[0], xs[1] = halves(x_ref[...].T)
-        phis[0], phis[1] = halves(phi[...].T)
+        store_upper(xs_l, xs_r, halves(x_ref[...].T))
+        store_upper(phis_l, phis_r, halves(phi[...].T))
         solved = lower_times(inverse, halves(raw[...].reshape(2 * PIVOT, PIVOT)), ((1,), (1,)))
         q = halves(solved[:, :PIVOT])
-        qs[0], qs[1] = q
-        qds[0], qds[1] = halves(
-            solved[:, PIVOT:] - lower_times(halves(phi[...]), q, ((1,), (0,)))
+        store_stacked(qs.at[: 3 * PIVOT], q)
+        store_stacked(
+            qs.at[3 * PIVOT :],
+            halves(solved[:, PIVOT:] - lower_times(halves(phi[...]), q, ((1,), (0,)))),
         )
 
     for shift, part, tangent_part in zip((0, 3, 1, 2), parts, tangent_parts):
@@ -258,21 +281,19 @@
             high, low = halves(value)
             rows_ref[0, at : at + PANEL_TILE, lanes] = high
             rows_ref[1, at : at + PANEL_TILE, lanes] = low
-    solved = times_upper([rows_ref[0], rows_ref[1]], [xs[0], xs[1]])
+    solved = times_upper([rows_ref[0], rows_ref[1]], xs_l, xs_r)
     factor = solved[:PANEL_TILE]
     factor_halves = halves(factor)
-    change = solved[PANEL_TILE:] - times_upper(factor_halves, [phis[0], phis[1]])
-    change_halves = halves(change)
+    change = solved[PANEL_TILE:] - times_upper(factor_halves, phis_l, phis_r)
     done_ref[0] = factor
     done_ref[1] = change
     lanes = pl.ds(pl.multiple_of(col * 128, 128), 128)
     panel_out[...] = done_ref[0, :, lanes]
     panel_change_out[...] = done_ref[1, :, lanes]
-    q = [qs[0], qs[1]]
-    strip_out[...] = strip_ref[...] - split_product(factor_halves, q)
-    strip_change_out[...] = strip_tangent_ref[...] - (
-        split_product(change_halves, q) + split_product(factor_halves, [qds[0], qds[1]])
-    )
+    by_factor = end_to_end(factor_halves)
+    strip_out[...] = strip_ref[...] - product(by_factor, qs[: 3 * PIVOT], ((1,), (0,)))
+    by_both = jnp.concatenate([end_to_end(halves(change)), by_factor], axis=1)
+    strip_change_out[...] = strip_tangent_ref[...] - product(by_both, qs[...], ((1,), (0,)))
 
 
 def row_index(x, z, core):
@@ -317,7 +338,7 @@
 LIMIT = pltpu.CompilerParams(vmem_limit_bytes=56 * 2**20)
 
 
-def run_panel(at, whole_factor, inverse, rest_pieces, parts, tangent_parts, strip_block, strip_tangent):
+def run_panel(at, own_factor, inverse, rest_pieces, parts, tangent_parts, strip_block, strip_tangent):
     local_rows, local_strip = strip_block.shape
     tile = PANEL_TILE
     narrow = pl.BlockSpec((tile, 128), lambda i: (i, 0))
@@ -325,7 +346,6 @@
     corner = pl.BlockSpec((8, 128), lambda i: (0, 0))
     stacked = lambda which: pl.BlockSpec((None, tile, 128), lambda i: (which, i, 0))
     square = pltpu.VMEM((PIVOT, PIVOT), F32)
-    split_square = pltpu.VMEM((2, PIVOT, PIVOT), BF16)
     return pl.pallas_call(
         panel,
         name="panel",
@@ -338,7 +358,7 @@
             matrix(local_rows, local_strip),
             matrix(local_rows, local_strip),
         ),
-        in_specs=[smem_spec()] + [vmem_spec()] * 10 + [narrow, *[stacked(0)] * 3]
+        in_specs=[smem_spec()] + [vmem_spec()] * 11 + [narrow, *[stacked(0)] * 3]
         + [narrow, *[stacked(1)] * 3]
         + [broad] * 2,
         out_specs=(corner, corner, narrow, narrow, broad, broad),
@@ -346,16 +366,18 @@
             square,
             pltpu.VMEM((2, PIVOT, PIVOT), F32),
             square,
-            split_square,
-            split_square,
-            split_square,
-            split_square,
+            pltpu.VMEM((3 * HALF, HALF), BF16),
+            pltpu.VMEM((3 * PIVOT, HALF), BF16),
+            pltpu.VMEM((3 * HALF, HALF), BF16),
+            pltpu.VMEM((3 * PIVOT, HALF), BF16),
+            pltpu.VMEM((6 * PIVOT, PIVOT), BF16),
             pltpu.VMEM((2, 2 * tile, PIVOT), BF16),
             pltpu.VMEM((2, tile, PIVOT), F32),
+            square,
         ],
         compiler_params=LIMIT,
         cost_estimate=pl.CostEstimate(flops=10**10, bytes_accessed=20 * 10**6, transcendentals=0),
-    )(at, whole_factor, inverse, *rest_pieces, *parts, *tangent_parts, strip_block, strip_tangent)
+    )(at, own_factor, *inverse, *rest_pieces, *parts, *tangent_parts, strip_block, strip_tangent)
 
 
 def body(pivot_block, pivot_tangent, panel_block, panel_tangent, strip_block, strip_tangent):
@@ -389,29 +411,32 @@
     tangent_parts = [panel_tangent, left, right, far]
 
     quarter = matrix(HALF, HALF)
-    factored = pl.pallas_call(
+    small = matrix(BLOCK, BLOCK)
+    x_first, *factored = pl.pallas_call(
         first_blocks,
         name="first_blocks",
-        out_shape=(quarter, matrix(PIVOT, HALF), quarter, quarter, quarter),
+        out_shape=(quarter, quarter, matrix(8, HALF), small, matrix(HALF, BLOCK), small),
         in_specs=[smem_spec()] + [vmem_spec()] * 8 + [pl.BlockSpec(memory_space=pl.ANY)],
-        out_specs=[vmem_spec()] * 5,
-        scratch_shapes=[pltpu.VMEM((PIVOT, PIVOT), F32)],
+        out_specs=[vmem_spec()] * 6,
+        scratch_shapes=[pltpu.VMEM((PIVOT, PIVOT), F32), pltpu.VMEM((PIVOT, HALF), F32)]
+        + [pltpu.VMEM((HALF, HALF), F32)] * 3,
         compiler_params=LIMIT,
         cost_estimate=pl.CostEstimate(flops=22 * 10**9, bytes_accessed=10**6, transcendentals=0),
     )(at, *pivot_pieces, right)
-    whole_factor, inverse = pl.pallas_call(
+    own_factor, x_low = pl.pallas_call(
         last_block,
         name="last_block",
-        out_shape=(matrix(PIVOT, PIVOT), matrix(PIVOT, PIVOT)),
-        in_specs=[vmem_spec()] * 5,
+        out_shape=(matrix(8, PIVOT), matrix(HALF, PIVOT)),
+        in_specs=[smem_spec()] + [vmem_spec()] * 5,
         out_specs=[vmem_spec()] * 2,
-        scratch_shapes=[pltpu.VMEM((HALF, HALF), F32)] * 2,
+        scratch_shapes=[pltpu.VMEM((HALF, HALF), F32)] * 3,
         compiler_params=LIMIT,
         cost_estimate=pl.CostEstimate(flops=10 * 10**9, bytes_accessed=10**6, transcendentals=0),
-    )(*factored)
+    )(at, *factored)
+    inverse = (x_first, x_low)
 
     return run_panel(
-        at, whole_factor, inverse, rest_pieces, parts, tangent_parts, strip_block, strip_tangent
+        at, own_factor, inverse, rest_pieces, parts, tangent_parts, strip_block, strip_tangent
     )
 
 

time: 103 us -> 101 us (0.981)
  Pallas kernels: 45.6 us -> 43.8 us
    pallas_call x2, Pallas kernels: 24.2 us -> 22.8 us  [the longest x1 16.6 us: body(): pl.pallas_call(first_blocks, name='first_blocks', out_shape=(quarter, qua...]
  transfers between devices with their start and end apart: 21 -> 21, of which waited for: 5 -> 5; matrix products, arithmetic and copies ran while one was open for 1% -> 1% of each run, Pallas kernels for 24% -> 23%
where the time goes in v3:
time: 101 us
  Pallas kernels  43.8 us (43%)
  starting transfers between devices  30.1 us (30%)
  waiting for transfers between devices  20.9 us (21%)
  local copies, waits for them, and re-layouts  3.26 us (3%)
  other arithmetic  1.4 us (1%)
  between operations  1.12 us (1%)
    pallas_call x1, Pallas kernels, run_panel(): pl.pallas_call(panel, name='panel', grid=(local_rows // tile,), out_shape...  21 us
    pallas_call x1, Pallas kernels, body(): pl.pallas_call(first_blocks, name='first_blocks', out_shape=(quarter, qua...  16.6 us
    ppermute x14, starting transfers between devices, along_x_core(): return lax.ppermute(value, 'row', pairs)  13.3 us
    all_to_all x1, waiting for transfers between devices, gather_z(): return lax.all_to_all(spread, 'row', 0, 0, axis_index_groups=ALONG_Z)  12.3 us
    ppermute x6, starting transfers between devices, along_y(): return lax.ppermute(value, 'col', [(c, (c + s) % N_Y) for c in range(N_Y)])  8.56 us
    all_to_all x1, starting transfers between devices, gather_z(): return lax.all_to_all(spread, 'row', 0, 0, axis_index_groups=ALONG_Z)  8.19 us
    ppermute x6, waiting for transfers between devices, along_y(): return lax.ppermute(value, 'col', [(c, (c + s) % N_Y) for c in range(N_Y)])  6.65 us
    pallas_call x1, Pallas kernels, body(): pl.pallas_call(last_block, name='last_block', out_shape=(matrix(8, PIVOT)...  6.2 us
  transfers between devices with their start and end apart: 21, of which 5 were waited for; matrix products, arithmetic and copies ran while one was open for 1% of the time, Pallas kernels for 23%

profile of v3, /device:TPU:1, one launch (start us, length us, event | category | flops | bytes accessed | tf_op | source)
XLA Modules:
  0.0 100.6 jit_solution(2100203987680480067)
XLA Ops:
  0.6 0.0 copy-start
  0.6 0.0 copy-start.1
  0.7 0.9 dynamic-slice_bitcast_fusion.6
  1.6 0.7 maximum_bitcast_fusion
  2.3 2.1 %collective-permute-start = (f32[4,8,128]{2,1,0:T(8,128)S(1)}, f32[4,8,128]{2,1,0:T(8,128)S(1)}, u32[]{:S(2)}, u32[]{:S(2)}) collective-permute-start(f32[4,8,128]{2,1,0:T(8,128)S(1)} %get-tuple-element.31), channel_id=1, source_target_pairs={{0,1},{1,2},{2,3},{3,0},{4,5},{5,6},{6,7},{7,4},{8,9},{9,10},{10,1... | collective-permute-start | bytes 49160 | tf_op jit(solution)/shard_map/ppermute | solution.py:308
  4.4 2.6 %collective-permute-start.1 = (f32[4,8,128]{2,1,0:T(8,128)S(1)}, f32[4,8,128]{2,1,0:T(8,128)S(1)}, u32[]{:S(2)}, u32[]{:S(2)}) collective-permute-start(f32[4,8,128]{2,1,0:T(8,128)S(1)} %get-tuple-element.32), channel_id=1, source_target_pairs={{0,2},{1,3},{2,0},{3,1},{4,6},{5,7},{6,4},{7,5},{8,10},{9,11},{10,... | collective-permute-start | bytes 49160 | tf_op jit(solution)/shard_map/ppermute | solution.py:308
  7.0 1.1 %collective-permute-start.2 = (f32[4,8,128]{2,1,0:T(8,128)S(1)}, f32[4,8,128]{2,1,0:T(8,128)S(1)}, u32[]{:S(2)}, u32[]{:S(2)}) collective-permute-start(f32[4,8,128]{2,1,0:T(8,128)S(1)} %get-tuple-element.33), channel_id=1, source_target_pairs={{0,3},{1,0},{2,1},{3,2},{4,7},{5,4},{6,5},{7,6},{8,11},{9,8},{10,9... | collective-permute-start | bytes 49160 | tf_op jit(solution)/shard_map/ppermute | solution.py:308
  8.1 0.4 collective-permute-done.1
  8.5 1.4 %collective-permute-done.2 = f32[4,8,128]{2,1,0:T(8,128)S(1)} collective-permute-done((f32[4,8,128]{2,1,0:T(8,128)S(1)}, f32[4,8,128]{2,1,0:T(8,128)S(1)}, u32[]{:S(2)}, u32[]{:S(2)}) %collective-permute-start.2) | collective-permute-done | bytes 16416 | tf_op jit(solution)/shard_map/ppermute | solution.py:308
  9.9 0.9 broadcast_in_dim.2
  10.8 8.2 %all-to-all-start = ((f32[8,4,4,8,128]{4,3,2,1,0:T(8,128)}), f32[8,4,4,8,128]{4,3,2,1,0:T(8,128)S(1)}, u32[]{:S(2)}, u32[]{:S(2)}) async-start(f32[8,4,4,8,128]{4,3,2,1,0:T(8,128)} %broadcast_in_dim.2), calls=%async_computation | async-start | bytes 1048576 | tf_op jit(solution)/shard_map/all_to_all | solution.py:323
  19.0 0.1 pad_maximum_fusion
  19.0 0.1 collective-permute-start.18
  19.1 2.7 %collective-permute-start.10 = (f32[2,1024,128]{2,1,0:T(8,128)S(1)}, f32[2,1024,128]{2,1,0:T(8,128)}, u32[]{:S(2)}, u32[]{:S(2)}) collective-permute-start(f32[2,1024,128]{2,1,0:T(8,128)S(1)} %pad_maximum_fusion), channel_id=1, source_target_pairs={{0,3},{1,0},{2,1},{3,2},{4,7},{5,4},{6,5},{7,6},{8,11},{9,8},{10,9... | collective-permute-start | bytes 3145736 | tf_op jit(solution)/shard_map/ppermute | solution.py:308
  21.8 12.3 %all-to-all-done = f32[8,4,4,8,128]{4,3,2,1,0:T(8,128)S(1)} async-done(((f32[8,4,4,8,128]{4,3,2,1,0:T(8,128)}), f32[8,4,4,8,128]{4,3,2,1,0:T(8,128)S(1)}, u32[]{:S(2)}, u32[]{:S(2)}) %all-to-all-start) | async-done | bytes 524320 | tf_op jit(solution)/shard_map/all_to_all | solution.py:323
  34.1 0.0 copy-start.3
  34.1 2.6 %collective-permute-start.5 = (f32[8,4,8,128]{3,2,1,0:T(8,128)S(1)}, f32[8,4,8,128]{3,2,1,0:T(8,128)S(1)}, u32[]{:S(2)}, u32[]{:S(2)}) collective-permute-start(f32[8,4,8,128]{3,2,1,0:T(8,128)S(1)} %slice_bitcast_fusion.refs_1_), channel_id=1, source_target_pairs={{0,192},{4,196},{8,200},{12,204},{16,208},{20,212},{24,216},{28,22... | collective-permute-start | bytes 393224 | tf_op jit(solution)/shard_map/ppermute | solution.py:318
  36.7 0.5 collective-permute-start.4
  37.2 0.6 collective-permute-start.3
  37.8 4.8 %collective-permute-done.18.refs_13_.refs_17_ = f32[2,1024,128]{2,1,0:T(8,128)S(1)} collective-permute-done((f32[2,1024,128]{2,1,0:T(8,128)S(1)}, f32[2,1024,128]{2,1,0:T(8,128)S(1)}, u32[]{:S(2)}, u32[]{:S(2)}) %collective-permute-start.18) | collective-permute-done | bytes 1048608 | tf_op jit(solution)/shard_map/ppermute | solution.py:308
  42.6 3.3 %collective-permute-start.6 = (f32[8,4,8,128]{3,2,1,0:T(8,128)S(1)}, f32[8,4,8,128]{3,2,1,0:T(8,128)S(1)}, u32[]{:S(2)}, u32[]{:S(2)}) collective-permute-start(f32[8,4,8,128]{3,2,1,0:T(8,128)S(1)} %slice_bitcast_fusion.refs_1_), channel_id=1, source_target_pairs={{0,4},{4,0},{8,12},{12,8},{16,20},{20,16},{24,28},{28,24},{32,36},... | collective-permute-start | bytes 393224 | tf_op jit(solution)/shard_map/ppermute | solution.py:318
  45.9 0.1 collective-permute-start.9
  46.0 0.0 collective-permute-done.4.refs_3_
  46.0 0.8 collective-permute-start.8
  46.8 1.3 %collective-permute-start.7 = (f32[8,4,8,128]{3,2,1,0:T(8,128)S(1)}, f32[8,4,8,128]{3,2,1,0:T(8,128)}, u32[]{:S(2)}, u32[]{:S(2)}) collective-permute-start(f32[8,4,8,128]{3,2,1,0:T(8,128)S(1)} %collective-permute-done.3.refs_2_), channel_id=1, source_target_pairs={{0,4},{4,0},{8,12},{12,8},{16,20},{20,16},{24,28},{28,24},{32,36},... | collective-permute-start | bytes 393224 | tf_op jit(solution)/shard_map/ppermute | solution.py:318
  48.2 0.6 pad_add_fusion.refs_0_.at_ref
  48.8 0.0 collective-permute-done.10.refs_9_.refs_14_.refs_18_
  48.8 0.1 collective-permute-start.14
  48.9 1.3 %collective-permute-start.13 = (f32[8,4,3,8,128]{4,3,2,1,0:T(8,128)S(1)}, f32[8,4,3,8,128]{4,3,2,1,0:T(8,128)S(1)}, u32[]{:S(2)}, u32[]{:S(2)}) collective-permute-start(f32[8,4,3,8,128]{4,3,2,1,0:T(8,128)S(1)} %slice.9.refs_4_), channel_id=1, source_target_pairs={{0,192},{4,196},{8,200},{12,204},{16,208},{20,212},{24,216},{28,22... | collective-permute-start | bytes 1179656 | tf_op jit(solution)/shard_map/ppermute | solution.py:318
  50.2 0.0 collective-permute-done.9.refs_8_
  50.2 0.5 collective-permute-start.12
  50.8 0.0 collective-permute-done.8.refs_7_
  50.8 0.6 collective-permute-start.11
  51.4 0.0 collective-permute-done.7.refs_6_
  51.4 0.0 collective-permute-start.19
  51.4 16.6 %first_blocks.1 = (f32[256,256]{1,0:T(8,128)}, f32[256,256]{1,0:T(8,128)}, f32[8,256]{1,0:T(8,128)}, f32[128,128]{1,0:T(8,128)}, f32[256,128]{1,0:T(8,128)}, /*index=5*/f32[128,128]{1,0:T(8,128)}) custom-call(s32[4]{0:T(128)} %pad_add_fusion.refs_0_.at_ref, f32[8,4,8,128]{3,2,1,0:T(8,128)} %copy-done.3, f32[8,4,8,128]{3,2,1,0:T(8,128)} %copy-done.15, ...), custom_call_target="tpu_custom_call" | custom-call | flops 22000001024 | bytes 1000000 | tf_op jit(solution)/shard_map/first_blocks/pallas_call | solution.py:415
  68.1 0.0 collective-permute-done.13.refs_7_
  68.1 1.0 collective-permute-start.17
  69.1 0.1 collective-permute-start.16
  69.2 2.0 %collective-permute-done.11.refs_5_ = f32[8,4,3,8,128]{4,3,2,1,0:T(8,128)S(1)} collective-permute-done((f32[8,4,3,8,128]{4,3,2,1,0:T(8,128)S(1)}, f32[8,4,3,8,128]{4,3,2,1,0:T(8,128)S(1)}, u32[]{:S(2)}, u32[]{:S(2)}) %collective-permute-start.11) | collective-permute-done | bytes 393248 | tf_op jit(solution)/shard_map/ppermute | solution.py:318
  71.2 0.5 collective-permute-start.15
  71.7 6.2 %last_block.1 = (f32[8,512]{1,0:T(8,128)}, f32[256,512]{1,0:T(8,128)}) custom-call(s32[4]{0:T(128)} %pad_add_fusion.refs_0_.at_ref, f32[256,256]{1,0:T(8,128)} %get-tuple-element.14.t_in, f32[8,256]{1,0:T(8,128)} %get-tuple-element.15.own_left, f32[128,128]{1,0:T(8,128)} %get-tuple-element.16.w_last, f32[256,128]{1,0:T(8,128)} %get-tuple-element.17.l_low, ...), custom_call_target="tpu_custom_call" | custom-call | flops 10000000000 | bytes 1000000 | tf_op jit(solution)/shard_map/last_block/pallas_call | solution.py:426
  78.0 0.7 copy-done.6
  78.7 0.1 copy-done.10
  78.8 0.1 copy-done.11
  79.0 0.1 copy-done.12
  79.1 0.3 copy-done.5
  79.4 21.0 %panel.1 = (f32[8,128]{1,0:T(8,128)}, f32[8,128]{1,0:T(8,128)}, f32[1024,128]{1,0:T(8,128)}, f32[1024,128]{1,0:T(8,128)}, f32[1024,512]{1,0:T(8,128)}, /*index=5*/f32[1024,512]{1,0:T(8,128)}) custom-call(s32[4]{0:T(128)} %pad_add_fusion.refs_0_.at_ref, f32[8,512]{1,0:T(8,128)} %get-tuple-element.19.refs_1_, f32[256,256]{1,0:T(8,128)} %get-tuple-element.20.refs_2_, ...), custom_call_target="tpu_custom_call" | custom-call | flops 10000000000 | bytes 20000000 | tf_op jit(solution)/shard_map/panel/pallas_call | solution.py:349
  (43 shorter events, 0.1 us)
Async XLA Ops:
  0.6 18.3 %copy-start = (f32[1024,128]{1,0:T(8,128)S(1)}, f32[1024,128]{1,0:T(8,128)}, u32[]{:S(2)}) copy-start(f32[1024,128]{1,0:T(8,128)} %refs_16_.1) | copy-start | bytes 1572868
  0.6 18.3 %copy-start.1 = (f32[1024,128]{1,0:T(8,128)S(1)}, f32[1024,128]{1,0:T(8,128)}, u32[]{:S(2)}) copy-start(f32[1024,128]{1,0:T(8,128)} %refs_12_.1) | copy-start | bytes 1572868
  2.3 5.8 %collective-permute-start = (f32[4,8,128]{2,1,0:T(8,128)S(1)}, f32[4,8,128]{2,1,0:T(8,128)S(1)}, u32[]{:S(2)}, u32[]{:S(2)}) collective-permute-start(f32[4,8,128]{2,1,0:T(8,128)S(1)} %get-tuple-element.31), channel_id=1, source_target_pairs={{0,1},{1,2},{2,3},{3,0},{4,5},{5,6},{6,7},{7,4},{8,9},{9,10},{10,1... | collective-permute-start | bytes 49160 | tf_op jit(solution)/shard_map/ppermute | solution.py:308
  4.4 4.1 %collective-permute-start.1 = (f32[4,8,128]{2,1,0:T(8,128)S(1)}, f32[4,8,128]{2,1,0:T(8,128)S(1)}, u32[]{:S(2)}, u32[]{:S(2)}) collective-permute-start(f32[4,8,128]{2,1,0:T(8,128)S(1)} %get-tuple-element.32), channel_id=1, source_target_pairs={{0,2},{1,3},{2,0},{3,1},{4,6},{5,7},{6,4},{7,5},{8,10},{9,11},{10,... | collective-permute-start | bytes 49160 | tf_op jit(solution)/shard_map/ppermute | solution.py:308
  7.0 2.9 %collective-permute-start.2 = (f32[4,8,128]{2,1,0:T(8,128)S(1)}, f32[4,8,128]{2,1,0:T(8,128)S(1)}, u32[]{:S(2)}, u32[]{:S(2)}) collective-permute-start(f32[4,8,128]{2,1,0:T(8,128)S(1)} %get-tuple-element.33), channel_id=1, source_target_pairs={{0,3},{1,0},{2,1},{3,2},{4,7},{5,4},{6,5},{7,6},{8,11},{9,8},{10,9... | collective-permute-start | bytes 49160 | tf_op jit(solution)/shard_map/ppermute | solution.py:308
  10.8 23.3 %all-to-all-start = ((f32[8,4,4,8,128]{4,3,2,1,0:T(8,128)}), f32[8,4,4,8,128]{4,3,2,1,0:T(8,128)S(1)}, u32[]{:S(2)}, u32[]{:S(2)}) async-start(f32[8,4,4,8,128]{4,3,2,1,0:T(8,128)} %broadcast_in_dim.2), calls=%async_computation | async-start | bytes 1048576 | tf_op jit(solution)/shard_map/all_to_all | solution.py:323
  19.0 23.6 %collective-permute-start.18 = (f32[2,1024,128]{2,1,0:T(8,128)S(1)}, f32[2,1024,128]{2,1,0:T(8,128)S(1)}, u32[]{:S(2)}, u32[]{:S(2)}) collective-permute-start(f32[2,1024,128]{2,1,0:T(8,128)S(1)} %pad_maximum_fusion), channel_id=1, source_target_pairs={{0,1},{1,2},{2,3},{3,0},{4,5},{5,6},{6,7},{7,4},{8,9},{9,10},{10,1... | collective-permute-start | bytes 3145736 | tf_op jit(solution)/shard_map/ppermute | solution.py:308
  19.1 29.7 %collective-permute-start.10 = (f32[2,1024,128]{2,1,0:T(8,128)S(1)}, f32[2,1024,128]{2,1,0:T(8,128)}, u32[]{:S(2)}, u32[]{:S(2)}) collective-permute-start(f32[2,1024,128]{2,1,0:T(8,128)S(1)} %pad_maximum_fusion), channel_id=1, source_target_pairs={{0,3},{1,0},{2,1},{3,2},{4,7},{5,4},{6,5},{7,6},{8,11},{9,8},{10,9... | collective-permute-start | bytes 3145736 | tf_op jit(solution)/shard_map/ppermute | solution.py:308
  34.1 17.3 %copy-start.3 = (f32[8,4,8,128]{3,2,1,0:T(8,128)}, f32[8,4,8,128]{3,2,1,0:T(8,128)S(1)}, u32[]{:S(2)}) copy-start(f32[8,4,8,128]{3,2,1,0:T(8,128)S(1)} %slice_bitcast_fusion.refs_1_) | copy-start | bytes 393220
  34.1 11.8 %collective-permute-start.5 = (f32[8,4,8,128]{3,2,1,0:T(8,128)S(1)}, f32[8,4,8,128]{3,2,1,0:T(8,128)S(1)}, u32[]{:S(2)}, u32[]{:S(2)}) collective-permute-start(f32[8,4,8,128]{3,2,1,0:T(8,128)S(1)} %slice_bitcast_fusion.refs_1_), channel_id=1, source_target_pairs={{0,192},{4,196},{8,200},{12,204},{16,208},{20,212},{24,216},{28,22... | collective-permute-start | bytes 393224 | tf_op jit(solution)/shard_map/ppermute | solution.py:318
  36.7 9.4 %collective-permute-start.4 = (f32[8,4,8,128]{3,2,1,0:T(8,128)S(1)}, f32[8,4,8,128]{3,2,1,0:T(8,128)S(1)}, u32[]{:S(2)}, u32[]{:S(2)}) collective-permute-start(f32[8,4,8,128]{3,2,1,0:T(8,128)S(1)} %slice_bitcast_fusion.refs_1_), channel_id=1, source_target_pairs={{0,128},{4,132},{8,136},{12,140},{16,144},{20,148},{24,152},{28,15... | collective-permute-start | bytes 393224 | tf_op jit(solution)/shard_map/ppermute | solution.py:318
  37.2 9.7 %collective-permute-start.3 = (f32[8,4,8,128]{3,2,1,0:T(8,128)S(1)}, f32[8,4,8,128]{3,2,1,0:T(8,128)S(1)}, u32[]{:S(2)}, u32[]{:S(2)}) collective-permute-start(f32[8,4,8,128]{3,2,1,0:T(8,128)S(1)} %slice_bitcast_fusion.refs_1_), channel_id=1, source_target_pairs={{0,64},{4,68},{8,72},{12,76},{16,80},{20,84},{24,88},{28,92},{32,9... | collective-permute-start | bytes 393224 | tf_op jit(solution)/shard_map/ppermute | solution.py:318
  42.6 25.4 %copy-start.4 = (f32[2,1024,128]{2,1,0:T(8,128)}, f32[2,1024,128]{2,1,0:T(8,128)S(1)}, u32[]{:S(2)}) copy-start(f32[2,1024,128]{2,1,0:T(8,128)S(1)} %collective-permute-done.18.refs_13_.refs_17_) | copy-start | bytes 3145732
  42.6 6.3 %collective-permute-start.6 = (f32[8,4,8,128]{3,2,1,0:T(8,128)S(1)}, f32[8,4,8,128]{3,2,1,0:T(8,128)S(1)}, u32[]{:S(2)}, u32[]{:S(2)}) collective-permute-start(f32[8,4,8,128]{3,2,1,0:T(8,128)S(1)} %slice_bitcast_fusion.refs_1_), channel_id=1, source_target_pairs={{0,4},{4,0},{8,12},{12,8},{16,20},{20,16},{24,28},{28,24},{32,36},... | collective-permute-start | bytes 393224 | tf_op jit(solution)/shard_map/ppermute | solution.py:318
  45.9 5.5 %copy-start.13 = (f32[8,4,8,128]{3,2,1,0:T(8,128)}, f32[8,4,8,128]{3,2,1,0:T(8,128)S(1)}, u32[]{:S(2)}) copy-start(f32[8,4,8,128]{3,2,1,0:T(8,128)S(1)} %collective-permute-done.5.refs_4_) | copy-start | bytes 393220
  45.9 4.3 %collective-permute-start.9 = (f32[8,4,8,128]{3,2,1,0:T(8,128)S(1)}, f32[8,4,8,128]{3,2,1,0:T(8,128)S(1)}, u32[]{:S(2)}, u32[]{:S(2)}) collective-permute-start(f32[8,4,8,128]{3,2,1,0:T(8,128)S(1)} %collective-permute-done.5.refs_4_), channel_id=1, source_target_pairs={{0,4},{4,0},{8,12},{12,8},{16,20},{20,16},{24,28},{28,24},{32,36},... | collective-permute-start | bytes 393224 | tf_op jit(solution)/shard_map/ppermute | solution.py:318
  46.0 5.4 %copy-start.14 = (f32[8,4,8,128]{3,2,1,0:T(8,128)}, f32[8,4,8,128]{3,2,1,0:T(8,128)S(1)}, u32[]{:S(2)}) copy-start(f32[8,4,8,128]{3,2,1,0:T(8,128)S(1)} %collective-permute-done.4.refs_3_) | copy-start | bytes 393220
  46.0 4.7 %collective-permute-start.8 = (f32[8,4,8,128]{3,2,1,0:T(8,128)S(1)}, f32[8,4,8,128]{3,2,1,0:T(8,128)S(1)}, u32[]{:S(2)}, u32[]{:S(2)}) collective-permute-start(f32[8,4,8,128]{3,2,1,0:T(8,128)S(1)} %collective-permute-done.4.refs_3_), channel_id=1, source_target_pairs={{0,4},{4,0},{8,12},{12,8},{16,20},{20,16},{24,28},{28,24},{32,36},... | collective-permute-start | bytes 393224 | tf_op jit(solution)/shard_map/ppermute | solution.py:318
  46.8 4.6 %copy-start.15 = (f32[8,4,8,128]{3,2,1,0:T(8,128)}, f32[8,4,8,128]{3,2,1,0:T(8,128)S(1)}, u32[]{:S(2)}) copy-start(f32[8,4,8,128]{3,2,1,0:T(8,128)S(1)} %collective-permute-done.3.refs_2_) | copy-start | bytes 393220
  46.8 4.5 %collective-permute-start.7 = (f32[8,4,8,128]{3,2,1,0:T(8,128)S(1)}, f32[8,4,8,128]{3,2,1,0:T(8,128)}, u32[]{:S(2)}, u32[]{:S(2)}) collective-permute-start(f32[8,4,8,128]{3,2,1,0:T(8,128)S(1)} %collective-permute-done.3.refs_2_), channel_id=1, source_target_pairs={{0,4},{4,0},{8,12},{12,8},{16,20},{20,16},{24,28},{28,24},{32,36},... | collective-permute-start | bytes 393224 | tf_op jit(solution)/shard_map/ppermute | solution.py:318
  48.8 19.3 %copy-start.2 = (f32[8,4,3,8,128]{4,3,2,1,0:T(8,128)}, f32[8,4,3,8,128]{4,3,2,1,0:T(8,128)S(1)}, u32[]{:S(2)}) copy-start(f32[8,4,3,8,128]{4,3,2,1,0:T(8,128)S(1)} %slice.9.refs_4_) | copy-start | bytes 1179652
  48.8 29.1 %collective-permute-start.14 = (f32[8,4,3,8,128]{4,3,2,1,0:T(8,128)S(1)}, f32[8,4,3,8,128]{4,3,2,1,0:T(8,128)S(1)}, u32[]{:S(2)}, u32[]{:S(2)}) collective-permute-start(f32[8,4,3,8,128]{4,3,2,1,0:T(8,128)S(1)} %slice.9.refs_4_), channel_id=1, source_target_pairs={{0,4},{4,0},{8,12},{12,8},{16,20},{20,16},{24,28},{28,24},{32,36},... | collective-permute-start | bytes 1179656 | tf_op jit(solution)/shard_map/ppermute | solution.py:318
  48.9 2.5 %copy-start.16 = (f32[8,4,8,128]{3,2,1,0:T(8,128)}, f32[8,4,8,128]{3,2,1,0:T(8,128)S(1)}, u32[]{:S(2)}) copy-start(f32[8,4,8,128]{3,2,1,0:T(8,128)S(1)} %collective-permute-done.6.refs_5_) | copy-start | bytes 393220
  48.9 19.1 %collective-permute-start.13 = (f32[8,4,3,8,128]{4,3,2,1,0:T(8,128)S(1)}, f32[8,4,3,8,128]{4,3,2,1,0:T(8,128)S(1)}, u32[]{:S(2)}, u32[]{:S(2)}) collective-permute-start(f32[8,4,3,8,128]{4,3,2,1,0:T(8,128)S(1)} %slice.9.refs_4_), channel_id=1, source_target_pairs={{0,192},{4,196},{8,200},{12,204},{16,208},{20,212},{24,216},{28,22... | collective-permute-start | bytes 1179656 | tf_op jit(solution)/shard_map/ppermute | solution.py:318
  50.2 1.2 %copy-start.17 = (f32[8,4,8,128]{3,2,1,0:T(8,128)}, f32[8,4,8,128]{3,2,1,0:T(8,128)S(1)}, u32[]{:S(2)}) copy-start(f32[8,4,8,128]{3,2,1,0:T(8,128)S(1)} %collective-permute-done.9.refs_8_) | copy-start | bytes 393220
  50.2 18.9 %collective-permute-start.12 = (f32[8,4,3,8,128]{4,3,2,1,0:T(8,128)S(1)}, f32[8,4,3,8,128]{4,3,2,1,0:T(8,128)S(1)}, u32[]{:S(2)}, u32[]{:S(2)}) collective-permute-start(f32[8,4,3,8,128]{4,3,2,1,0:T(8,128)S(1)} %slice.9.refs_4_), channel_id=1, source_target_pairs={{0,128},{4,132},{8,136},{12,140},{16,144},{20,148},{24,152},{28,15... | collective-permute-start | bytes 1179656 | tf_op jit(solution)/shard_map/ppermute | solution.py:318
  50.8 0.7 copy-start.18
  50.8 20.4 %collective-permute-start.11 = (f32[8,4,3,8,128]{4,3,2,1,0:T(8,128)S(1)}, f32[8,4,3,8,128]{4,3,2,1,0:T(8,128)S(1)}, u32[]{:S(2)}, u32[]{:S(2)}) collective-permute-start(f32[8,4,3,8,128]{4,3,2,1,0:T(8,128)S(1)} %slice.9.refs_4_), channel_id=1, source_target_pairs={{0,64},{4,68},{8,72},{12,76},{16,80},{20,84},{24,88},{28,92},{32,9... | collective-permute-start | bytes 1179656 | tf_op jit(solution)/shard_map/ppermute | solution.py:318
  51.4 26.6 %collective-permute-start.19 = (f32[2,1024,128]{2,1,0:T(8,128)S(1)}, f32[2,1024,128]{2,1,0:T(8,128)S(1)}, u32[]{:S(2)}, u32[]{:S(2)}) collective-permute-start(f32[2,1024,128]{2,1,0:T(8,128)S(1)} %collective-permute-done.18.refs_13_.refs_17_), channel_id=1, source_target_pairs={{0,1},{1,2},{2,3},{3,0},{4,5},{5,6},{6,7},{7,4},{8,9},{9,10},{10,1... | collective-permute-start | bytes 3145736 | tf_op jit(solution)/shard_map/ppermute | solution.py:308
  68.1 9.8 %copy-start.7 = (f32[8,4,3,8,128]{4,3,2,1,0:T(8,128)}, f32[8,4,3,8,128]{4,3,2,1,0:T(8,128)S(1)}, u32[]{:S(2)}) copy-start(f32[8,4,3,8,128]{4,3,2,1,0:T(8,128)S(1)} %collective-permute-done.13.refs_7_) | copy-start | bytes 1179652
  68.1 9.8 %collective-permute-start.17 = (f32[8,4,3,8,128]{4,3,2,1,0:T(8,128)S(1)}, f32[8,4,3,8,128]{4,3,2,1,0:T(8,128)S(1)}, u32[]{:S(2)}, u32[]{:S(2)}) collective-permute-start(f32[8,4,3,8,128]{4,3,2,1,0:T(8,128)S(1)} %collective-permute-done.13.refs_7_), channel_id=1, source_target_pairs={{0,4},{4,0},{8,12},{12,8},{16,20},{20,16},{24,28},{28,24},{32,36},... | collective-permute-start | bytes 1179656 | tf_op jit(solution)/shard_map/ppermute | solution.py:318
  69.1 8.8 %copy-start.8 = (f32[8,4,3,8,128]{4,3,2,1,0:T(8,128)}, f32[8,4,3,8,128]{4,3,2,1,0:T(8,128)S(1)}, u32[]{:S(2)}) copy-start(f32[8,4,3,8,128]{4,3,2,1,0:T(8,128)S(1)} %collective-permute-done.12.refs_6_) | copy-start | bytes 1179652
  69.1 8.8 %collective-permute-start.16 = (f32[8,4,3,8,128]{4,3,2,1,0:T(8,128)S(1)}, f32[8,4,3,8,128]{4,3,2,1,0:T(8,128)S(1)}, u32[]{:S(2)}, u32[]{:S(2)}) collective-permute-start(f32[8,4,3,8,128]{4,3,2,1,0:T(8,128)S(1)} %collective-permute-done.12.refs_6_), channel_id=1, source_target_pairs={{0,4},{4,0},{8,12},{12,8},{16,20},{20,16},{24,28},{28,24},{32,36},... | collective-permute-start | bytes 1179656 | tf_op jit(solution)/shard_map/ppermute | solution.py:318
  71.2 6.7 %copy-start.9 = (f32[8,4,3,8,128]{4,3,2,1,0:T(8,128)}, f32[8,4,3,8,128]{4,3,2,1,0:T(8,128)S(1)}, u32[]{:S(2)}) copy-start(f32[8,4,3,8,128]{4,3,2,1,0:T(8,128)S(1)} %collective-permute-done.11.refs_5_) | copy-start | bytes 1179652
  71.2 6.8 %collective-permute-start.15 = (f32[8,4,3,8,128]{4,3,2,1,0:T(8,128)S(1)}, f32[8,4,3,8,128]{4,3,2,1,0:T(8,128)S(1)}, u32[]{:S(2)}, u32[]{:S(2)}) collective-permute-start(f32[8,4,3,8,128]{4,3,2,1,0:T(8,128)S(1)} %collective-permute-done.11.refs_5_), channel_id=1, source_target_pairs={{0,4},{4,0},{8,12},{12,8},{16,20},{20,16},{24,28},{28,24},{32,36},... | collective-permute-start | bytes 1179656 | tf_op jit(solution)/shard_map/ppermute | solution.py:318
  77.9 0.7 copy-start.6
  77.9 0.9 copy-start.10
  78.0 1.0 copy-start.11
  78.0 1.1 %copy-start.12 = (f32[8,4,3,8,128]{4,3,2,1,0:T(8,128)}, f32[8,4,3,8,128]{4,3,2,1,0:T(8,128)S(1)}, u32[]{:S(2)}) copy-start(f32[8,4,3,8,128]{4,3,2,1,0:T(8,128)S(1)} %collective-permute-done.15.refs_9_) | copy-start | bytes 1179652
  78.0 1.4 %copy-start.5 = (f32[2,1024,128]{2,1,0:T(8,128)}, f32[2,1024,128]{2,1,0:T(8,128)S(1)}, u32[]{:S(2)}) copy-start(f32[2,1024,128]{2,1,0:T(8,128)S(1)} %collective-permute-done.19.refs_15_.refs_19_) | copy-start | bytes 3145732
